TPU v7x, 512 devices: a whole 4x8x8 slice. The times are simulated.
512 devices in a mesh: probe: 8 (over y_lo, core), space: 64 (over y_hi, x, z).
Axes of the slice: x: 4, y: 8 (y_hi: 2, y_lo: 4; y = y_hi * 4 + y_lo), z: 8, core: 2. Of those that a mesh axis runs over, the one named last changes fastest.
Arguments:
- probe_dirs: float32 [32, 64, 256], P('probe', 'space'), may hold values from -6 to 6
- log_param: float32 [64, 256], P('space'), may hold values from -1 to 1
- background: float32 [512, 32, 512], P('space'), may hold values from 0.3 to 1.5
- site_class: int32 [512, 32, 512], P('space'), may hold values from 0 to 3
- trap_density: float32 [4], replicated, may hold values from 0.2 to 1
Outputs:
- q_basis: float32 [32, 64, 256], P('probe', 'space')
- lower_factor: float32 [32, 32], replicated
All inputs are finite; a program needn't handle non-finite values.
Results may differ from a plain program's by a relative error of at most 0.0003.
Values sent between devices are 32-bit elements; how exact they have to be, the bound alone decides.
A program may use at most 64 MiB of HBM per device.

v0:
```python
import jax
import jax.numpy as jnp
from jax import lax
from jax.sharding import PartitionSpec as P

PX = 64
PY = 4
REF = 8
STEPS = 4


TIME_STEP = 0.12


def padded_2(x, sides, width):
    for axis, dim in sides:
        count, length = (lax.axis_size(axis), x.shape[dim])
        up = [(i, (i + 1) % count) for i in range(count - 1)]
        down = [(j, i) for i, j in up]
        last = lax.slice_in_dim(x, length - width, length, axis=dim)
        first = lax.slice_in_dim(x, 0, width, axis=dim)
        before = lax.ppermute(last, axis, up)
        after = lax.ppermute(first, axis, down)
        x = jnp.concatenate([before, x, after], axis=dim)
    return x


def lower_solve(factor, rows):
    return lax.linalg.triangular_solve(factor, rows, left_side=True, lower=True)


def prolong(coarse):
    leading = coarse.shape[:-2]
    planes = coarse.shape[-2]
    coarse_grid = coarse.reshape(leading + (planes, PY, PX))
    expanded = jnp.broadcast_to(
        coarse_grid[..., :, None, :, None, :, None], leading + (planes, REF, PY, REF, PX, REF)
    )
    return expanded.reshape(leading + (planes * REF, PY * REF, PX * REF))


def restrict(finegrid):
    probe_count = finegrid.shape[0]
    planes = finegrid.shape[1] // REF
    shaped = finegrid.reshape((probe_count, planes, REF, PY, REF, PX, REF))
    return jnp.sum(shaped, axis=(2, 4, 6)).reshape((probe_count, planes, PY * PX))


def stencil(padded, current, trap_rate):
    up_down = padded[:, 2:, :, :] + padded[:, :-2, :, :]
    flat_pad = jnp.pad(current, ((0, 0), (0, 0), (1, 1), (1, 1)))
    lateral = (
        flat_pad[:, :, 2:, 1:-1]
        + flat_pad[:, :, :-2, 1:-1]
        + flat_pad[:, :, 1:-1, 2:]
        + flat_pad[:, :, 1:-1, :-2]
    )
    return current + TIME_STEP * (up_down + lateral - 6.0 * current - trap_rate[None] * current)


def cholesky_pass(rows, gram_sum, cell_count):
    highest = lax.Precision.HIGHEST
    partial_gram = jnp.dot(rows, rows.T, precision=highest, preferred_element_type=jnp.float32)
    gram_matrix = gram_sum(partial_gram) / cell_count
    factor = jnp.linalg.cholesky(gram_matrix)
    return (lower_solve(factor, rows), factor)


def shards(probe_dirs, log_param, background, site_class, trap_density):
    probe_count = probe_dirs.shape[0]
    planes = probe_dirs.shape[1]
    plane_cells = probe_dirs.shape[2]
    density = jnp.zeros(site_class.shape, jnp.float32)
    for class_index in range(trap_density.shape[0]):
        density = density + jnp.where(site_class == class_index, trap_density[class_index], 0.0)
    trap_rate = density * jnp.exp(prolong(log_param))
    source = -TIME_STEP * trap_rate * background
    tangent = source[None] * prolong(probe_dirs)
    for step_index in range(STEPS - 1):
        padded = padded_2(tangent, (("space", 1),), 1)
        tangent = stencil(padded, tangent, trap_rate)
    adjoint = tangent
    summed = adjoint
    for step_index in range(STEPS - 1):
        padded = padded_2(adjoint, (("space", 1),), 1)
        adjoint = stencil(padded, adjoint, trap_rate)
        summed = summed + adjoint
    images = restrict(source[None] * summed).reshape((probe_count, planes * plane_cells))
    cell_count = float(planes * lax.axis_size("space") * plane_cells)
    highest = lax.Precision.HIGHEST
    every_probe = lax.all_gather(images, "probe", axis=0, tiled=True)

    def space_sum(partial_gram):
        return lax.psum(partial_gram, "space")

    basis_one, factor_one = cholesky_pass(every_probe, space_sum, cell_count)
    q_rows, factor_two = cholesky_pass(basis_one, space_sum, cell_count)
    q_local = lax.dynamic_slice_in_dim(
        q_rows, lax.axis_index("probe") * probe_count, probe_count, 0
    )
    lower_factor = jnp.dot(
        factor_one, factor_two, precision=highest, preferred_element_type=jnp.float32
    )
    return (q_local.reshape((probe_count, planes, plane_cells)), lower_factor)


def solution(mesh):
    placed = (
        P("probe", "space", None),
        P("space", None),
        P("space", None, None),
        P("space", None, None),
        P(),
    )
    return jax.shard_map(
        shards,
        mesh=mesh,
        in_specs=placed,
        out_specs=(P("probe", "space", None), P()),
        check_vma=False,
    )
```

profile of v0, /device:TPU:56, one launch (start us, length us, event | category | flops | bytes accessed | tf_op | source)
XLA Modules:
  0.0 1067.1 jit_solution(6931667937898231620)
XLA Ops:
  3.7 2.5 broadcast_in_dim.55
  6.2 4.1 broadcast_in_dim.56
  10.3 2.8 multiply_multiply_fusion.2
  13.4 15.4 %collective-permute-start = (f32[4,1,32,512]{3,2,1,0:T(8,128)S(1)}, f32[4,1,32,512]{3,2,1,0:T(8,128)S(1)}, u32[]{:S(2)}, u32[]{:S(2)}) collective-permute-start(f32[4,1,32,512]{3,2,1,0:T(8,128)S(1)} %get-tuple-element.16), channel_id=1, source_target_pairs={{1,0},{2,1},{3,2},{4,3},{5,4},{6,5},{7,6},{8,7},{9,8},{10,9},{11,1... | collective-permute-start | bytes 786440 | tf_op jit(solution)/shard_map/ppermute | solution.py:23
  30.7 3.6 collective-permute-done
  34.3 12.3 %collective-permute-done.1 = f32[4,1,32,512]{3,2,1,0:T(8,128)S(1)} collective-permute-done((f32[4,1,32,512]{3,2,1,0:T(8,128)S(1)}, f32[4,1,32,512]{3,2,1,0:T(8,128)S(1)}, u32[]{:S(2)}, u32[]{:S(2)}) %collective-permute-start.1) | collective-permute-done | bytes 262176 | tf_op jit(solution)/shard_map/ppermute | solution.py:22
  51.0 3.9 collective-permute-start.3
  54.9 2.8 collective-permute-done.2
  57.8 10.2 collective-permute-done.3
  67.9 2.5 fusion.14
  72.4 3.9 collective-permute-start.5
  76.3 2.4 collective-permute-done.4
  78.7 10.1 collective-permute-done.5
  88.8 2.5 fusion.22
  93.2 3.9 collective-permute-start.7
  99.6 10.1 collective-permute-done.7
  114.0 3.9 collective-permute-start.9
  120.3 10.1 collective-permute-done.9
  130.4 2.5 fusion.38
  137.0 4.1 collective-permute-start.11
  141.1 2.5 collective-permute-done.10
  143.6 10.1 collective-permute-done.11
  153.8 10.9 %fusion.55 = f32[4,32,512]{2,1,0:T(8,128)} fusion(f32[4,8,32,512]{3,2,1,0:T(8,128)} %copy-done, f32[4,1,32,512]{3,2,1,0:T(8,128)} %collective-permute-done.11, f32[4,1,32,512]{3,2,1,0:T(8,128)} %collective-permute-done.10, f32[4,8,32,512]{3,2,1,0:T(8,128)S(1)} %fusion.22, f32[8,32,512]{2,1,0:T(8,128)S(1)} %get-tuple-element.5, ...), kind=kLoop, calls=%fused_computation.94 | loop fusion | flops 16187392 | bytes 6553600 | tf_op jit(solution)/shard_map/reduce_sum | solution.py:46
  164.7 4.5 reduce_sum.14
  169.2 2.6 reduce_sum.18
  171.8 22.3 %all-gather = f32[8,4,256]{2,1,0:T(4,128)S(1)} all-gather(f32[1,4,256]{2,1,0:T(4,128)S(1)} %reshape.39), channel_id=1, replica_groups=mesh['probe'=8,'space'=64] {'probe'}, dimensions={0}, use_global_device_ids=true | all-gather | bytes 36864 | tf_op jit(solution)/shard_map/all_gather | solution.py:91
  194.3 427.9 %psum.14 = f32[32,32]{0,1:T(8,128)S(1)} all-reduce(f32[32,32]{0,1:T(8,128)S(1)} %fusion.84), channel_id=1, replica_groups=mesh['probe'=8,'space'=64] {'space'}, use_global_device_ids=true, to_apply=%region_2.3 | all-reduce | flops 1024 | bytes 8192 | tf_op jit(solution)/shard_map/psum | solution.py:94
  622.2 2.9 cholesky.44
  626.5 2.4 custom-call.6
  629.3 427.9 %psum.15 = f32[32,32]{0,1:T(8,128)S(1)} all-reduce(f32[32,32]{0,1:T(8,128)S(1)} %fusion.85), channel_id=1, replica_groups=mesh['probe'=8,'space'=64] {'space'}, use_global_device_ids=true, to_apply=%region_5.8 | all-reduce | flops 1024 | bytes 8192 | tf_op jit(solution)/shard_map/psum | solution.py:94
  1057.3 2.9 cholesky.55
  1063.8 2.4 custom-call.7
  (55 shorter events, 33.3 us)
Async XLA Ops:
  0.6 2.9 copy-start.4
  6.2 4.1 copy-start.2
  6.2 4.1 copy-start.3
  13.4 20.9 %collective-permute-start = (f32[4,1,32,512]{3,2,1,0:T(8,128)S(1)}, f32[4,1,32,512]{3,2,1,0:T(8,128)S(1)}, u32[]{:S(2)}, u32[]{:S(2)}) collective-permute-start(f32[4,1,32,512]{3,2,1,0:T(8,128)S(1)} %get-tuple-element.16), channel_id=1, source_target_pairs={{1,0},{2,1},{3,2},{4,3},{5,4},{6,5},{7,6},{8,7},{9,8},{10,9},{11,1... | collective-permute-start | bytes 786440 | tf_op jit(solution)/shard_map/ppermute | solution.py:23
  28.8 17.9 %collective-permute-start.1 = (f32[4,1,32,512]{3,2,1,0:T(8,128)S(1)}, f32[4,1,32,512]{3,2,1,0:T(8,128)S(1)}, u32[]{:S(2)}, u32[]{:S(2)}) collective-permute-start(f32[4,1,32,512]{3,2,1,0:T(8,128)S(1)} %get-tuple-element.17), channel_id=1, source_target_pairs={{0,1},{1,2},{2,3},{3,4},{4,5},{5,6},{6,7},{7,8},{8,9},{9,10},{10,1... | collective-permute-start | bytes 786440 | tf_op jit(solution)/shard_map/ppermute | solution.py:22
  49.1 8.7 collective-permute-start.2
  51.0 16.9 %collective-permute-start.3 = (f32[4,1,32,512]{3,2,1,0:T(8,128)S(1)}, f32[4,1,32,512]{3,2,1,0:T(8,128)S(1)}, u32[]{:S(2)}, u32[]{:S(2)}) collective-permute-start(f32[4,1,32,512]{3,2,1,0:T(8,128)S(1)} %get-tuple-element.15), channel_id=1, source_target_pairs={{0,1},{1,2},{2,3},{3,4},{4,5},{5,6},{6,7},{7,8},{8,9},{9,10},{10,1... | collective-permute-start | bytes 786440 | tf_op jit(solution)/shard_map/ppermute | solution.py:22
  70.4 8.3 collective-permute-start.4
  72.4 16.4 %collective-permute-start.5 = (f32[4,1,32,512]{3,2,1,0:T(8,128)S(1)}, f32[4,1,32,512]{3,2,1,0:T(8,128)S(1)}, u32[]{:S(2)}, u32[]{:S(2)}) collective-permute-start(f32[4,1,32,512]{3,2,1,0:T(8,128)S(1)} %get-tuple-element.13), channel_id=1, source_target_pairs={{0,1},{1,2},{2,3},{3,4},{4,5},{5,6},{6,7},{7,8},{8,9},{9,10},{10,1... | collective-permute-start | bytes 786440 | tf_op jit(solution)/shard_map/ppermute | solution.py:22
  91.3 8.3 collective-permute-start.6
  93.2 16.4 %collective-permute-start.7 = (f32[4,1,32,512]{3,2,1,0:T(8,128)S(1)}, f32[4,1,32,512]{3,2,1,0:T(8,128)S(1)}, u32[]{:S(2)}, u32[]{:S(2)}) collective-permute-start(f32[4,1,32,512]{3,2,1,0:T(8,128)S(1)} %get-tuple-element.11), channel_id=1, source_target_pairs={{0,1},{1,2},{2,3},{3,4},{4,5},{5,6},{6,7},{7,8},{8,9},{9,10},{10,1... | collective-permute-start | bytes 786440 | tf_op jit(solution)/shard_map/ppermute | solution.py:22
  109.6 2.4 copy-start.1
  112.0 8.3 collective-permute-start.8
  114.0 16.4 %collective-permute-start.9 = (f32[4,1,32,512]{3,2,1,0:T(8,128)S(1)}, f32[4,1,32,512]{3,2,1,0:T(8,128)S(1)}, u32[]{:S(2)}, u32[]{:S(2)}) collective-permute-start(f32[4,1,32,512]{3,2,1,0:T(8,128)S(1)} %get-tuple-element.9), channel_id=1, source_target_pairs={{0,1},{1,2},{2,3},{3,4},{4,5},{5,6},{6,7},{7,8},{8,9},{9,10},{10,1... | collective-permute-start | bytes 786440 | tf_op jit(solution)/shard_map/ppermute | solution.py:22
  132.8 1.4 copy-start
  135.0 8.6 collective-permute-start.10
  137.0 16.8 %collective-permute-start.11 = (f32[4,1,32,512]{3,2,1,0:T(8,128)}, f32[4,1,32,512]{3,2,1,0:T(8,128)}, u32[]{:S(2)}, u32[]{:S(2)}) collective-permute-start(f32[4,1,32,512]{3,2,1,0:T(8,128)} %get-tuple-element.7), channel_id=1, source_target_pairs={{0,1},{1,2},{2,3},{3,4},{4,5},{5,6},{6,7},{7,8},{8,9},{9,10},{10,1... | collective-permute-start | bytes 786440 | tf_op jit(solution)/shard_map/ppermute | solution.py:22
where the time goes:
time: 1070 us
  blocking collectives  878 us (82%)
  waiting for transfers between devices  79 us (7%)
  starting transfers between devices  46.7 us (4%)
  other arithmetic  42.2 us (4%)
  local copies, waits for them, and re-layouts  17.3 us (2%)
    psum x2, blocking collectives, space_sum(): return lax.psum(partial_gram, 'space')  856 us
    ppermute x6, waiting for transfers between devices, padded_2(): before = lax.ppermute(last, axis, up)  62.8 us
    ppermute x6, starting transfers between devices, padded_2(): after = lax.ppermute(first, axis, down)  25 us
    all_gather x1, blocking collectives, shards(): every_probe = lax.all_gather(images, 'probe', axis=0, tiled=True)  22.3 us
    ppermute x6, starting transfers between devices, padded_2(): before = lax.ppermute(last, axis, up)  21.7 us
  transfers between devices with their start and end apart: 12, of which 12 were waited for; matrix products, arithmetic and copies ran while one was open for 0% of the time, Pallas kernels for 0%

commit v1 on v0

--- a/solution.py
+++ b/solution.py
@@ -91,7 +91,13 @@
     every_probe = lax.all_gather(images, "probe", axis=0, tiled=True)
 
     def space_sum(partial_gram):
-        return lax.psum(partial_gram, "space")
+        count = lax.axis_size("space")
+        distance = 1
+        while distance < count:
+            swap = [(i, i ^ distance) for i in range(count)]
+            partial_gram = partial_gram + lax.ppermute(partial_gram, "space", swap)
+            distance *= 2
+        return partial_gram
 
     basis_one, factor_one = cholesky_pass(every_probe, space_sum, cell_count)
     q_rows, factor_two = cholesky_pass(basis_one, space_sum, cell_count)

time: 1070 us -> 291 us (0.27)
  blocking collectives: 878 us -> 22.3 us
  waiting for transfers between devices: 79 us -> 143 us
  starting transfers between devices: 46.7 us -> 70.2 us
    psum x2 -> x0, blocking collectives: 856 us -> none  [space_sum(): return lax.psum(partial_gram, 'space')]
    ppermute x0 -> x12, waiting for transfers between devices: none -> 64.4 us  [space_sum(): partial_gram = partial_gram + lax.ppermute(partial_gram, 'space', swap)]
    ppermute x0 -> x12, starting transfers between devices: none -> 23.5 us  [space_sum(): partial_gram = partial_gram + lax.ppermute(partial_gram, 'space', swap)]
  transfers between devices with their start and end apart: 12 -> 24, of which waited for: 12 -> 24; matrix products, arithmetic and copies ran while one was open for 0% -> 0% of each run, Pallas kernels for 0% -> 0%
where the time goes in v1:
time: 291 us; the launch traced here: 290 us
  waiting for transfers between devices  143 us (49%)
  starting transfers between devices  70.2 us (24%)
  other arithmetic  36.5 us (13%)
  blocking collectives  22.3 us (8%)
  local copies, waits for them, and re-layouts  14.4 us (5%)
    ppermute x12, waiting for transfers between devices, space_sum(): partial_gram = partial_gram + lax.ppermute(partial_gram, 'space', swap)  64.4 us
    ppermute x6, waiting for transfers between devices, padded_2(): before = lax.ppermute(last, axis, up)  62.7 us
    ppermute x6, starting transfers between devices, padded_2(): after = lax.ppermute(first, axis, down)  25 us
    ppermute x12, starting transfers between devices, space_sum(): partial_gram = partial_gram + lax.ppermute(partial_gram, 'space', swap)  23.5 us
    all_gather x1, blocking collectives, shards(): every_probe = lax.all_gather(images, 'probe', axis=0, tiled=True)  22.3 us
    ppermute x6, starting transfers between devices, padded_2(): before = lax.ppermute(last, axis, up)  21.7 us
    ppermute x6, waiting for transfers between devices, padded_2(): after = lax.ppermute(first, axis, down)  15.9 us
    add x5, other arithmetic, stencil(): current + TIME_STEP * (up_down + lateral - 6.0 * current - trap_rate[None...  12.2 us
  transfers between devices with their start and end apart: 24, of which 24 were waited for; matrix products, arithmetic and copies ran while one was open for 0% of the time, Pallas kernels for 0%

profile of v1, /device:TPU:56, one launch (start us, length us, event | category | flops | bytes accessed | tf_op | source)
XLA Modules:
  0.0 290.3 jit_solution(18005360073006245054)
XLA Ops:
  6.3 4.1 %broadcast_in_dim.56 = f32[4,32,512]{2,1,0:T(8,128)S(1)} reshape(f32[4,4,8,64,8]{4,3,2,1,0:T(8,128)} %broadcast_in_dim.55) | data formatting | bytes 524288 | tf_op jit(solution)/shard_map/broadcast_in_dim | solution.py:36
  13.5 15.4 %collective-permute-start = (f32[4,1,32,512]{3,2,1,0:T(8,128)S(1)}, f32[4,1,32,512]{3,2,1,0:T(8,128)S(1)}, u32[]{:S(2)}, u32[]{:S(2)}) collective-permute-start(f32[4,1,32,512]{3,2,1,0:T(8,128)S(1)} %get-tuple-element.16), channel_id=1, source_target_pairs={{1,0},{2,1},{3,2},{4,3},{5,4},{6,5},{7,6},{8,7},{9,8},{10,9},{11,1... | collective-permute-start | bytes 786440 | tf_op jit(solution)/shard_map/ppermute | solution.py:23
  30.8 3.6 %collective-permute-done = f32[4,1,32,512]{3,2,1,0:T(8,128)S(1)} collective-permute-done((f32[4,1,32,512]{3,2,1,0:T(8,128)S(1)}, f32[4,1,32,512]{3,2,1,0:T(8,128)S(1)}, u32[]{:S(2)}, u32[]{:S(2)}) %collective-permute-start) | collective-permute-done | bytes 262176 | tf_op jit(solution)/shard_map/ppermute | solution.py:23
  34.4 12.3 %collective-permute-done.1 = f32[4,1,32,512]{3,2,1,0:T(8,128)S(1)} collective-permute-done((f32[4,1,32,512]{3,2,1,0:T(8,128)S(1)}, f32[4,1,32,512]{3,2,1,0:T(8,128)S(1)}, u32[]{:S(2)}, u32[]{:S(2)}) %collective-permute-start.1) | collective-permute-done | bytes 262176 | tf_op jit(solution)/shard_map/ppermute | solution.py:22
  51.1 3.9 %collective-permute-start.3 = (f32[4,1,32,512]{3,2,1,0:T(8,128)S(1)}, f32[4,1,32,512]{3,2,1,0:T(8,128)S(1)}, u32[]{:S(2)}, u32[]{:S(2)}) collective-permute-start(f32[4,1,32,512]{3,2,1,0:T(8,128)S(1)} %get-tuple-element.15), channel_id=1, source_target_pairs={{0,1},{1,2},{2,3},{3,4},{4,5},{5,6},{6,7},{7,8},{8,9},{9,10},{10,1... | collective-permute-start | bytes 786440 | tf_op jit(solution)/shard_map/ppermute | solution.py:22
  55.1 2.8 collective-permute-done.2
  57.9 10.2 %collective-permute-done.3 = f32[4,1,32,512]{3,2,1,0:T(8,128)S(1)} collective-permute-done((f32[4,1,32,512]{3,2,1,0:T(8,128)S(1)}, f32[4,1,32,512]{3,2,1,0:T(8,128)S(1)}, u32[]{:S(2)}, u32[]{:S(2)}) %collective-permute-start.3) | collective-permute-done | bytes 262176 | tf_op jit(solution)/shard_map/ppermute | solution.py:22
  72.5 3.9 %collective-permute-start.5 = (f32[4,1,32,512]{3,2,1,0:T(8,128)S(1)}, f32[4,1,32,512]{3,2,1,0:T(8,128)S(1)}, u32[]{:S(2)}, u32[]{:S(2)}) collective-permute-start(f32[4,1,32,512]{3,2,1,0:T(8,128)S(1)} %get-tuple-element.13), channel_id=1, source_target_pairs={{0,1},{1,2},{2,3},{3,4},{4,5},{5,6},{6,7},{7,8},{8,9},{9,10},{10,1... | collective-permute-start | bytes 786440 | tf_op jit(solution)/shard_map/ppermute | solution.py:22
  78.9 10.1 %collective-permute-done.5 = f32[4,1,32,512]{3,2,1,0:T(8,128)S(1)} collective-permute-done((f32[4,1,32,512]{3,2,1,0:T(8,128)S(1)}, f32[4,1,32,512]{3,2,1,0:T(8,128)S(1)}, u32[]{:S(2)}, u32[]{:S(2)}) %collective-permute-start.5) | collective-permute-done | bytes 262176 | tf_op jit(solution)/shard_map/ppermute | solution.py:22
  93.4 3.9 %collective-permute-start.7 = (f32[4,1,32,512]{3,2,1,0:T(8,128)S(1)}, f32[4,1,32,512]{3,2,1,0:T(8,128)S(1)}, u32[]{:S(2)}, u32[]{:S(2)}) collective-permute-start(f32[4,1,32,512]{3,2,1,0:T(8,128)S(1)} %get-tuple-element.11), channel_id=1, source_target_pairs={{0,1},{1,2},{2,3},{3,4},{4,5},{5,6},{6,7},{7,8},{8,9},{9,10},{10,1... | collective-permute-start | bytes 786440 | tf_op jit(solution)/shard_map/ppermute | solution.py:22
  99.7 10.1 %collective-permute-done.7 = f32[4,1,32,512]{3,2,1,0:T(8,128)S(1)} collective-permute-done((f32[4,1,32,512]{3,2,1,0:T(8,128)S(1)}, f32[4,1,32,512]{3,2,1,0:T(8,128)S(1)}, u32[]{:S(2)}, u32[]{:S(2)}) %collective-permute-start.7) | collective-permute-done | bytes 262176 | tf_op jit(solution)/shard_map/ppermute | solution.py:22
  114.1 3.9 %collective-permute-start.9 = (f32[4,1,32,512]{3,2,1,0:T(8,128)S(1)}, f32[4,1,32,512]{3,2,1,0:T(8,128)S(1)}, u32[]{:S(2)}, u32[]{:S(2)}) collective-permute-start(f32[4,1,32,512]{3,2,1,0:T(8,128)S(1)} %get-tuple-element.9), channel_id=1, source_target_pairs={{0,1},{1,2},{2,3},{3,4},{4,5},{5,6},{6,7},{7,8},{8,9},{9,10},{10,1... | collective-permute-start | bytes 786440 | tf_op jit(solution)/shard_map/ppermute | solution.py:22
  120.4 10.1 %collective-permute-done.9 = f32[4,1,32,512]{3,2,1,0:T(8,128)S(1)} collective-permute-done((f32[4,1,32,512]{3,2,1,0:T(8,128)S(1)}, f32[4,1,32,512]{3,2,1,0:T(8,128)S(1)}, u32[]{:S(2)}, u32[]{:S(2)}) %collective-permute-start.9) | collective-permute-done | bytes 262176 | tf_op jit(solution)/shard_map/ppermute | solution.py:22
  135.0 4.1 %collective-permute-start.11 = (f32[4,1,32,512]{3,2,1,0:T(8,128)S(1)}, f32[4,1,32,512]{3,2,1,0:T(8,128)S(1)}, u32[]{:S(2)}, u32[]{:S(2)}) collective-permute-start(f32[4,1,32,512]{3,2,1,0:T(8,128)S(1)} %get-tuple-element.7), channel_id=1, source_target_pairs={{0,1},{1,2},{2,3},{3,4},{4,5},{5,6},{6,7},{7,8},{8,9},{9,10},{10,1... | collective-permute-start | bytes 786440 | tf_op jit(solution)/shard_map/ppermute | solution.py:22
  141.3 10.1 %collective-permute-done.11 = f32[4,1,32,512]{3,2,1,0:T(8,128)S(1)} collective-permute-done((f32[4,1,32,512]{3,2,1,0:T(8,128)S(1)}, f32[4,1,32,512]{3,2,1,0:T(8,128)S(1)}, u32[]{:S(2)}, u32[]{:S(2)}) %collective-permute-start.11) | collective-permute-done | bytes 262176 | tf_op jit(solution)/shard_map/ppermute | solution.py:22
  151.3 5.2 %fusion.55 = f32[4,32,512]{2,1,0:T(8,128)S(1)} fusion(f32[4,8,32,512]{3,2,1,0:T(8,128)S(1)} %fusion.38, f32[4,1,32,512]{3,2,1,0:T(8,128)S(1)} %collective-permute-done.11, f32[4,1,32,512]{3,2,1,0:T(8,128)S(1)} %collective-permute-done.10, f32[4,8,32,512]{3,2,1,0:T(8,128)S(1)} %fusion.22, f32[8,32,512]{2,1,0:T(8,128)S(1)} %get-tuple-element.5, ...), kind=kLoop, calls=%fused_computation.94 | loop fusion | flops 16187392 | bytes 6553600 | tf_op jit(solution)/shard_map/reduce_sum | solution.py:46
  156.6 3.6 %reduce_sum.14 = f32[4,4,8,64,8]{4,3,2,1,0:T(8,128)} reshape(f32[4,32,512]{2,1,0:T(8,128)S(1)} %fusion.55) | data formatting | bytes 524288 | tf_op jit(solution)/shard_map/reduce_sum | solution.py:46
  162.9 22.3 %all-gather = f32[8,4,256]{2,1,0:T(4,128)S(1)} all-gather(f32[1,4,256]{2,1,0:T(4,128)S(1)} %reshape.39), channel_id=1, replica_groups=mesh['probe'=8,'space'=64] {'probe'}, dimensions={0}, use_global_device_ids=true | all-gather | bytes 36864 | tf_op jit(solution)/shard_map/all_gather | solution.py:91
  187.3 3.7 %collective-permute-done.12 = f32[32,32]{0,1:T(8,128)S(1)} collective-permute-done((f32[32,32]{0,1:T(8,128)S(1)}, f32[32,32]{0,1:T(8,128)S(1)}, u32[]{:S(2)}, u32[]{:S(2)}) %collective-permute-start.12) | collective-permute-done | bytes 4128 | tf_op jit(solution)/shard_map/ppermute | solution.py:98
  192.9 4.6 %collective-permute-done.13 = f32[32,32]{0,1:T(8,128)S(1)} collective-permute-done((f32[32,32]{0,1:T(8,128)S(1)}, f32[32,32]{0,1:T(8,128)S(1)}, u32[]{:S(2)}, u32[]{:S(2)}) %collective-permute-start.13) | collective-permute-done | bytes 4128 | tf_op jit(solution)/shard_map/ppermute | solution.py:98
  199.4 7.6 %collective-permute-done.14 = f32[32,32]{0,1:T(8,128)S(1)} collective-permute-done((f32[32,32]{0,1:T(8,128)S(1)}, f32[32,32]{0,1:T(8,128)S(1)}, u32[]{:S(2)}, u32[]{:S(2)}) %collective-permute-start.14) | collective-permute-done | bytes 4128 | tf_op jit(solution)/shard_map/ppermute | solution.py:98
  209.0 3.7 %collective-permute-done.15 = f32[32,32]{0,1:T(8,128)S(1)} collective-permute-done((f32[32,32]{0,1:T(8,128)S(1)}, f32[32,32]{0,1:T(8,128)S(1)}, u32[]{:S(2)}, u32[]{:S(2)}) %collective-permute-start.15) | collective-permute-done | bytes 4128 | tf_op jit(solution)/shard_map/ppermute | solution.py:98
  214.6 5.2 %collective-permute-done.16 = f32[32,32]{0,1:T(8,128)S(1)} collective-permute-done((f32[32,32]{0,1:T(8,128)S(1)}, f32[32,32]{0,1:T(8,128)S(1)}, u32[]{:S(2)}, u32[]{:S(2)}) %collective-permute-start.16) | collective-permute-done | bytes 4128 | tf_op jit(solution)/shard_map/ppermute | solution.py:98
  221.7 7.6 %collective-permute-done.17 = f32[32,32]{0,1:T(8,128)S(1)} collective-permute-done((f32[32,32]{0,1:T(8,128)S(1)}, f32[32,32]{0,1:T(8,128)S(1)}, u32[]{:S(2)}, u32[]{:S(2)}) %collective-permute-start.17) | collective-permute-done | bytes 4128 | tf_op jit(solution)/shard_map/ppermute | solution.py:98
  229.4 2.9 %cholesky.44 = f32[32,32]{1,0:T(8,128)S(1)} custom-call(f32[32,32]{1,0:T(8,128)S(1)} %fusion.61), custom_call_target="Cholesky" | custom-call | tf_op jit(solution)/shard_map/jit(cholesky)/cholesky | solution.py:65
  238.5 3.7 %collective-permute-done.18 = f32[32,32]{0,1:T(8,128)S(1)} collective-permute-done((f32[32,32]{0,1:T(8,128)S(1)}, f32[32,32]{0,1:T(8,128)S(1)}, u32[]{:S(2)}, u32[]{:S(2)}) %collective-permute-start.18) | collective-permute-done | bytes 4128 | tf_op jit(solution)/shard_map/ppermute | solution.py:98
  244.1 4.7 %collective-permute-done.19 = f32[32,32]{0,1:T(8,128)S(1)} collective-permute-done((f32[32,32]{0,1:T(8,128)S(1)}, f32[32,32]{0,1:T(8,128)S(1)}, u32[]{:S(2)}, u32[]{:S(2)}) %collective-permute-start.19) | collective-permute-done | bytes 4128 | tf_op jit(solution)/shard_map/ppermute | solution.py:98
  250.9 7.4 %collective-permute-done.20 = f32[32,32]{0,1:T(8,128)S(1)} collective-permute-done((f32[32,32]{0,1:T(8,128)S(1)}, f32[32,32]{0,1:T(8,128)S(1)}, u32[]{:S(2)}, u32[]{:S(2)}) %collective-permute-start.20) | collective-permute-done | bytes 4128 | tf_op jit(solution)/shard_map/ppermute | solution.py:98
  260.3 3.6 %collective-permute-done.21 = f32[32,32]{0,1:T(8,128)S(1)} collective-permute-done((f32[32,32]{0,1:T(8,128)S(1)}, f32[32,32]{0,1:T(8,128)S(1)}, u32[]{:S(2)}, u32[]{:S(2)}) %collective-permute-start.21) | collective-permute-done | bytes 4128 | tf_op jit(solution)/shard_map/ppermute | solution.py:98
  265.9 5.1 %collective-permute-done.22 = f32[32,32]{0,1:T(8,128)S(1)} collective-permute-done((f32[32,32]{0,1:T(8,128)S(1)}, f32[32,32]{0,1:T(8,128)S(1)}, u32[]{:S(2)}, u32[]{:S(2)}) %collective-permute-start.22) | collective-permute-done | bytes 4128 | tf_op jit(solution)/shard_map/ppermute | solution.py:98
  273.1 7.5 %collective-permute-done.23 = f32[32,32]{0,1:T(8,128)S(1)} collective-permute-done((f32[32,32]{0,1:T(8,128)S(1)}, f32[32,32]{0,1:T(8,128)S(1)}, u32[]{:S(2)}, u32[]{:S(2)}) %collective-permute-start.23) | collective-permute-done | bytes 4128 | tf_op jit(solution)/shard_map/ppermute | solution.py:98
  280.7 2.9 %cholesky.55 = f32[32,32]{1,0:T(8,128)S(1)} custom-call(f32[32,32]{1,0:T(8,128)S(1)} %fusion.58), custom_call_target="Cholesky" | custom-call | tf_op jit(solution)/shard_map/jit(cholesky)/cholesky | solution.py:65
  (83 shorter events, 79.4 us)
Async XLA Ops:
  0.6 3.0 %copy-start.2 = (f32[4,1,256]{2,1,0:T(1,128)S(1)}, f32[4,1,256]{2,1,0:T(1,128)}, u32[]{:S(2)}) copy-start(f32[4,1,256]{2,1,0:T(1,128)} %param.8) | copy-start | bytes 12292
  6.3 4.1 %copy-start = (f32[8,32,512]{2,1,0:T(8,128)S(1)}, f32[8,32,512]{2,1,0:T(8,128)}, u32[]{:S(2)}) copy-start(f32[8,32,512]{2,1,0:T(8,128)} %param.10) | copy-start | bytes 1572868
  6.3 4.1 %copy-start.1 = (s32[8,32,512]{2,1,0:T(8,128)S(1)}, s32[8,32,512]{2,1,0:T(8,128)}, u32[]{:S(2)}) copy-start(s32[8,32,512]{2,1,0:T(8,128)} %param.11) | copy-start | bytes 1572868
  13.5 20.9 %collective-permute-start = (f32[4,1,32,512]{3,2,1,0:T(8,128)S(1)}, f32[4,1,32,512]{3,2,1,0:T(8,128)S(1)}, u32[]{:S(2)}, u32[]{:S(2)}) collective-permute-start(f32[4,1,32,512]{3,2,1,0:T(8,128)S(1)} %get-tuple-element.16), channel_id=1, source_target_pairs={{1,0},{2,1},{3,2},{4,3},{5,4},{6,5},{7,6},{8,7},{9,8},{10,9},{11,1... | collective-permute-start | bytes 786440 | tf_op jit(solution)/shard_map/ppermute | solution.py:23
  28.9 17.9 %collective-permute-start.1 = (f32[4,1,32,512]{3,2,1,0:T(8,128)S(1)}, f32[4,1,32,512]{3,2,1,0:T(8,128)S(1)}, u32[]{:S(2)}, u32[]{:S(2)}) collective-permute-start(f32[4,1,32,512]{3,2,1,0:T(8,128)S(1)} %get-tuple-element.17), channel_id=1, source_target_pairs={{0,1},{1,2},{2,3},{3,4},{4,5},{5,6},{6,7},{7,8},{8,9},{9,10},{10,1... | collective-permute-start | bytes 786440 | tf_op jit(solution)/shard_map/ppermute | solution.py:22
  49.2 8.7 %collective-permute-start.2 = (f32[4,1,32,512]{3,2,1,0:T(8,128)S(1)}, f32[4,1,32,512]{3,2,1,0:T(8,128)S(1)}, u32[]{:S(2)}, u32[]{:S(2)}) collective-permute-start(f32[4,1,32,512]{3,2,1,0:T(8,128)S(1)} %get-tuple-element.14), channel_id=1, source_target_pairs={{1,0},{2,1},{3,2},{4,3},{5,4},{6,5},{7,6},{8,7},{9,8},{10,9},{11,1... | collective-permute-start | bytes 786440 | tf_op jit(solution)/shard_map/ppermute | solution.py:23
  51.1 16.9 %collective-permute-start.3 = (f32[4,1,32,512]{3,2,1,0:T(8,128)S(1)}, f32[4,1,32,512]{3,2,1,0:T(8,128)S(1)}, u32[]{:S(2)}, u32[]{:S(2)}) collective-permute-start(f32[4,1,32,512]{3,2,1,0:T(8,128)S(1)} %get-tuple-element.15), channel_id=1, source_target_pairs={{0,1},{1,2},{2,3},{3,4},{4,5},{5,6},{6,7},{7,8},{8,9},{9,10},{10,1... | collective-permute-start | bytes 786440 | tf_op jit(solution)/shard_map/ppermute | solution.py:22
  70.6 8.3 %collective-permute-start.4 = (f32[4,1,32,512]{3,2,1,0:T(8,128)S(1)}, f32[4,1,32,512]{3,2,1,0:T(8,128)S(1)}, u32[]{:S(2)}, u32[]{:S(2)}) collective-permute-start(f32[4,1,32,512]{3,2,1,0:T(8,128)S(1)} %get-tuple-element.12), channel_id=1, source_target_pairs={{1,0},{2,1},{3,2},{4,3},{5,4},{6,5},{7,6},{8,7},{9,8},{10,9},{11,1... | collective-permute-start | bytes 786440 | tf_op jit(solution)/shard_map/ppermute | solution.py:23
  72.5 16.4 %collective-permute-start.5 = (f32[4,1,32,512]{3,2,1,0:T(8,128)S(1)}, f32[4,1,32,512]{3,2,1,0:T(8,128)S(1)}, u32[]{:S(2)}, u32[]{:S(2)}) collective-permute-start(f32[4,1,32,512]{3,2,1,0:T(8,128)S(1)} %get-tuple-element.13), channel_id=1, source_target_pairs={{0,1},{1,2},{2,3},{3,4},{4,5},{5,6},{6,7},{7,8},{8,9},{9,10},{10,1... | collective-permute-start | bytes 786440 | tf_op jit(solution)/shard_map/ppermute | solution.py:22
  91.4 8.3 %collective-permute-start.6 = (f32[4,1,32,512]{3,2,1,0:T(8,128)S(1)}, f32[4,1,32,512]{3,2,1,0:T(8,128)S(1)}, u32[]{:S(2)}, u32[]{:S(2)}) collective-permute-start(f32[4,1,32,512]{3,2,1,0:T(8,128)S(1)} %get-tuple-element.10), channel_id=1, source_target_pairs={{1,0},{2,1},{3,2},{4,3},{5,4},{6,5},{7,6},{8,7},{9,8},{10,9},{11,1... | collective-permute-start | bytes 786440 | tf_op jit(solution)/shard_map/ppermute | solution.py:23
  93.4 16.4 %collective-permute-start.7 = (f32[4,1,32,512]{3,2,1,0:T(8,128)S(1)}, f32[4,1,32,512]{3,2,1,0:T(8,128)S(1)}, u32[]{:S(2)}, u32[]{:S(2)}) collective-permute-start(f32[4,1,32,512]{3,2,1,0:T(8,128)S(1)} %get-tuple-element.11), channel_id=1, source_target_pairs={{0,1},{1,2},{2,3},{3,4},{4,5},{5,6},{6,7},{7,8},{8,9},{9,10},{10,1... | collective-permute-start | bytes 786440 | tf_op jit(solution)/shard_map/ppermute | solution.py:22
  112.2 8.3 %collective-permute-start.8 = (f32[4,1,32,512]{3,2,1,0:T(8,128)S(1)}, f32[4,1,32,512]{3,2,1,0:T(8,128)S(1)}, u32[]{:S(2)}, u32[]{:S(2)}) collective-permute-start(f32[4,1,32,512]{3,2,1,0:T(8,128)S(1)} %get-tuple-element.8), channel_id=1, source_target_pairs={{1,0},{2,1},{3,2},{4,3},{5,4},{6,5},{7,6},{8,7},{9,8},{10,9},{11,1... | collective-permute-start | bytes 786440 | tf_op jit(solution)/shard_map/ppermute | solution.py:23
  114.1 16.4 %collective-permute-start.9 = (f32[4,1,32,512]{3,2,1,0:T(8,128)S(1)}, f32[4,1,32,512]{3,2,1,0:T(8,128)S(1)}, u32[]{:S(2)}, u32[]{:S(2)}) collective-permute-start(f32[4,1,32,512]{3,2,1,0:T(8,128)S(1)} %get-tuple-element.9), channel_id=1, source_target_pairs={{0,1},{1,2},{2,3},{3,4},{4,5},{5,6},{6,7},{7,8},{8,9},{9,10},{10,1... | collective-permute-start | bytes 786440 | tf_op jit(solution)/shard_map/ppermute | solution.py:22
  133.0 8.3 %collective-permute-start.10 = (f32[4,1,32,512]{3,2,1,0:T(8,128)S(1)}, f32[4,1,32,512]{3,2,1,0:T(8,128)S(1)}, u32[]{:S(2)}, u32[]{:S(2)}) collective-permute-start(f32[4,1,32,512]{3,2,1,0:T(8,128)S(1)} %get-tuple-element.6), channel_id=1, source_target_pairs={{1,0},{2,1},{3,2},{4,3},{5,4},{6,5},{7,6},{8,7},{9,8},{10,9},{11,1... | collective-permute-start | bytes 786440 | tf_op jit(solution)/shard_map/ppermute | solution.py:23
  135.0 16.4 %collective-permute-start.11 = (f32[4,1,32,512]{3,2,1,0:T(8,128)S(1)}, f32[4,1,32,512]{3,2,1,0:T(8,128)S(1)}, u32[]{:S(2)}, u32[]{:S(2)}) collective-permute-start(f32[4,1,32,512]{3,2,1,0:T(8,128)S(1)} %get-tuple-element.7), channel_id=1, source_target_pairs={{0,1},{1,2},{2,3},{3,4},{4,5},{5,6},{6,7},{7,8},{8,9},{9,10},{10,1... | collective-permute-start | bytes 786440 | tf_op jit(solution)/shard_map/ppermute | solution.py:22
  185.4 5.6 %collective-permute-start.12 = (f32[32,32]{0,1:T(8,128)S(1)}, f32[32,32]{0,1:T(8,128)S(1)}, u32[]{:S(2)}, u32[]{:S(2)}) collective-permute-start(f32[32,32]{0,1:T(8,128)S(1)} %fusion.84), channel_id=1, source_target_pairs={{0,1},{1,0},{2,3},{3,2},{4,5},{5,4},{6,7},{7,6},{8,9},{9,8},{10,11... | collective-permute-start | bytes 12296 | tf_op jit(solution)/shard_map/ppermute | solution.py:98
  191.0 6.5 %collective-permute-start.13 = (f32[32,32]{0,1:T(8,128)S(1)}, f32[32,32]{0,1:T(8,128)S(1)}, u32[]{:S(2)}, u32[]{:S(2)}) collective-permute-start(f32[32,32]{0,1:T(8,128)S(1)} %add.227), channel_id=1, source_target_pairs={{0,2},{1,3},{2,0},{3,1},{4,6},{5,7},{6,4},{7,5},{8,10},{9,11},{10,... | collective-permute-start | bytes 12296 | tf_op jit(solution)/shard_map/ppermute | solution.py:98
  197.5 9.5 %collective-permute-start.14 = (f32[32,32]{0,1:T(8,128)S(1)}, f32[32,32]{0,1:T(8,128)S(1)}, u32[]{:S(2)}, u32[]{:S(2)}) collective-permute-start(f32[32,32]{0,1:T(8,128)S(1)} %add.228), channel_id=1, source_target_pairs={{0,4},{1,5},{2,6},{3,7},{4,0},{5,1},{6,2},{7,3},{8,12},{9,13},{10,... | collective-permute-start | bytes 12296 | tf_op jit(solution)/shard_map/ppermute | solution.py:98
  207.1 5.6 %collective-permute-start.15 = (f32[32,32]{0,1:T(8,128)S(1)}, f32[32,32]{0,1:T(8,128)S(1)}, u32[]{:S(2)}, u32[]{:S(2)}) collective-permute-start(f32[32,32]{0,1:T(8,128)S(1)} %add.229), channel_id=1, source_target_pairs={{0,8},{1,9},{2,10},{3,11},{4,12},{5,13},{6,14},{7,15},{8,0},{9,1},... | collective-permute-start | bytes 12296 | tf_op jit(solution)/shard_map/ppermute | solution.py:98
  212.7 7.1 %collective-permute-start.16 = (f32[32,32]{0,1:T(8,128)S(1)}, f32[32,32]{0,1:T(8,128)S(1)}, u32[]{:S(2)}, u32[]{:S(2)}) collective-permute-start(f32[32,32]{0,1:T(8,128)S(1)} %add.230), channel_id=1, source_target_pairs={{0,16},{1,17},{2,18},{3,19},{4,20},{5,21},{6,22},{7,23},{8,24},{9,... | collective-permute-start | bytes 12296 | tf_op jit(solution)/shard_map/ppermute | solution.py:98
  219.8 9.5 %collective-permute-start.17 = (f32[32,32]{0,1:T(8,128)S(1)}, f32[32,32]{0,1:T(8,128)S(1)}, u32[]{:S(2)}, u32[]{:S(2)}) collective-permute-start(f32[32,32]{0,1:T(8,128)S(1)} %add.231), channel_id=1, source_target_pairs={{0,32},{1,33},{2,34},{3,35},{4,36},{5,37},{6,38},{7,39},{8,40},{9,... | collective-permute-start | bytes 12296 | tf_op jit(solution)/shard_map/ppermute | solution.py:98
  236.6 5.6 %collective-permute-start.18 = (f32[32,32]{0,1:T(8,128)S(1)}, f32[32,32]{0,1:T(8,128)S(1)}, u32[]{:S(2)}, u32[]{:S(2)}) collective-permute-start(f32[32,32]{0,1:T(8,128)S(1)} %fusion.85), channel_id=1, source_target_pairs={{0,1},{1,0},{2,3},{3,2},{4,5},{5,4},{6,7},{7,6},{8,9},{9,8},{10,11... | collective-permute-start | bytes 12296 | tf_op jit(solution)/shard_map/ppermute | solution.py:98
  242.2 6.6 %collective-permute-start.19 = (f32[32,32]{0,1:T(8,128)S(1)}, f32[32,32]{0,1:T(8,128)S(1)}, u32[]{:S(2)}, u32[]{:S(2)}) collective-permute-start(f32[32,32]{0,1:T(8,128)S(1)} %add.233), channel_id=1, source_target_pairs={{0,2},{1,3},{2,0},{3,1},{4,6},{5,7},{6,4},{7,5},{8,10},{9,11},{10,... | collective-permute-start | bytes 12296 | tf_op jit(solution)/shard_map/ppermute | solution.py:98
  248.8 9.5 %collective-permute-start.20 = (f32[32,32]{0,1:T(8,128)S(1)}, f32[32,32]{0,1:T(8,128)S(1)}, u32[]{:S(2)}, u32[]{:S(2)}) collective-permute-start(f32[32,32]{0,1:T(8,128)S(1)} %add.234), channel_id=1, source_target_pairs={{0,4},{1,5},{2,6},{3,7},{4,0},{5,1},{6,2},{7,3},{8,12},{9,13},{10,... | collective-permute-start | bytes 12296 | tf_op jit(solution)/shard_map/ppermute | solution.py:98
  258.3 5.6 %collective-permute-start.21 = (f32[32,32]{0,1:T(8,128)S(1)}, f32[32,32]{0,1:T(8,128)S(1)}, u32[]{:S(2)}, u32[]{:S(2)}) collective-permute-start(f32[32,32]{0,1:T(8,128)S(1)} %add.235), channel_id=1, source_target_pairs={{0,8},{1,9},{2,10},{3,11},{4,12},{5,13},{6,14},{7,15},{8,0},{9,1},... | collective-permute-start | bytes 12296 | tf_op jit(solution)/shard_map/ppermute | solution.py:98
  263.9 7.1 %collective-permute-start.22 = (f32[32,32]{0,1:T(8,128)S(1)}, f32[32,32]{0,1:T(8,128)S(1)}, u32[]{:S(2)}, u32[]{:S(2)}) collective-permute-start(f32[32,32]{0,1:T(8,128)S(1)} %add.236), channel_id=1, source_target_pairs={{0,16},{1,17},{2,18},{3,19},{4,20},{5,21},{6,22},{7,23},{8,24},{9,... | collective-permute-start | bytes 12296 | tf_op jit(solution)/shard_map/ppermute | solution.py:98
  271.1 9.5 %collective-permute-start.23 = (f32[32,32]{0,1:T(8,128)S(1)}, f32[32,32]{0,1:T(8,128)S(1)}, u32[]{:S(2)}, u32[]{:S(2)}) collective-permute-start(f32[32,32]{0,1:T(8,128)S(1)} %add.237), channel_id=1, source_target_pairs={{0,32},{1,33},{2,34},{3,35},{4,36},{5,37},{6,38},{7,39},{8,40},{9,... | collective-permute-start | bytes 12296 | tf_op jit(solution)/shard_map/ppermute | solution.py:98

commit v2 on v0

--- a/solution.py
+++ b/solution.py
@@ -1,6 +1,8 @@
 import jax
 import jax.numpy as jnp
 from jax import lax
+from jax.experimental import pallas as pl
+from jax.experimental.pallas import tpu as pltpu
 from jax.sharding import PartitionSpec as P
 
 PX = 64
@@ -25,10 +27,6 @@
     return x
 
 
-def lower_solve(factor, rows):
-    return lax.linalg.triangular_solve(factor, rows, left_side=True, lower=True)
-
-
 def prolong(coarse):
     leading = coarse.shape[:-2]
     planes = coarse.shape[-2]
@@ -58,12 +56,151 @@
     return current + TIME_STEP * (up_down + lateral - 6.0 * current - trap_rate[None] * current)
 
 
-def cholesky_pass(rows, gram_sum, cell_count):
-    highest = lax.Precision.HIGHEST
-    partial_gram = jnp.dot(rows, rows.T, precision=highest, preferred_element_type=jnp.float32)
-    gram_matrix = gram_sum(partial_gram) / cell_count
-    factor = jnp.linalg.cholesky(gram_matrix)
-    return (lower_solve(factor, rows), factor)
+def dot_highest(a, b, contract):
+    return lax.dot_general(
+        a, b, (contract, ((), ())), precision=lax.Precision.HIGHEST,
+        preferred_element_type=jnp.float32,
+    )
+
+
+def factor_and_inverse(gram):
+    n = gram.shape[0]
+    row_at = lax.broadcasted_iota(jnp.int32, (n, 2 * n), 0)
+    lane_at = lax.broadcasted_iota(jnp.int32, (n, 2 * n), 1)
+    factor_row = lax.broadcasted_iota(jnp.int32, (n, n), 0)
+    factor_lane = lax.broadcasted_iota(jnp.int32, (n, n), 1)
+    work = jnp.concatenate([gram, jnp.zeros((n, n), jnp.float32)], axis=1)
+    work = work + jnp.where(lane_at == row_at + n, 1.0, 0.0)
+    factor = jnp.zeros((n, n), jnp.float32)
+    for j in range(n):
+        scale = lax.rsqrt(work[j : j + 1, j : j + 1])
+        row = work[j : j + 1, :] * scale
+        column = work[:, j : j + 1] * scale
+        keep = (factor_lane == j) & (factor_row >= j)
+        factor = jnp.where(keep, jnp.broadcast_to(column, (n, n)), factor)
+        work = jnp.where(
+            row_at > j, work - column * row, jnp.where(row_at == j, row, work)
+        )
+    return factor, work[:, n:]
+
+
+GROUP = 8
+
+
+def orthogonalize_kernel(
+    cell_count, images_ref, q_ref, lower_ref, gathered, rows, grams, image_send, image_recv,
+    gram_send, gram_recv,
+):
+    mesh_id = pl.DeviceIdType.MESH
+    me = lax.axis_index("probe")
+    place = lax.axis_index("space")
+    inner, outer = lax.rem(place, GROUP), lax.div(place, GROUP)
+
+    def probe_peer(k):
+        return {"probe": lax.rem(me + k, GROUP)}
+
+    def inner_peer(k):
+        return {"space": outer * GROUP + lax.rem(inner + k, GROUP)}
+
+    def outer_peer(k):
+        return {"space": lax.rem(outer + k, GROUP) * GROUP + inner}
+
+    barrier = pltpu.get_barrier_semaphore()
+    for peer in (probe_peer, inner_peer, outer_peer):
+        for k in range(1, GROUP):
+            pl.semaphore_signal(barrier, inc=1, device_id=peer(k), device_id_type=mesh_id)
+    pl.semaphore_wait(barrier, 3 * (GROUP - 1))
+
+    def send(src, dst, send_sem, recv_sem, device):
+        return pltpu.make_async_remote_copy(
+            src_ref=src, dst_ref=dst, send_sem=send_sem, recv_sem=recv_sem,
+            device_id=device, device_id_type=mesh_id,
+        )
+
+    copies = []
+    for k in range(1, GROUP):
+        copy = send(
+            images_ref, gathered.at[me], image_send.at[k], image_recv.at[me], probe_peer(k)
+        )
+        copy.start()
+        copies.append(copy)
+    gathered[me] = images_ref[...]
+    for k in range(1, GROUP):
+        slot = lax.rem(me + k, GROUP)
+        send(
+            images_ref, gathered.at[slot], image_send.at[k], image_recv.at[slot], probe_peer(k)
+        ).wait_recv()
+    count = images_ref.shape[0]
+    for slot in range(GROUP):
+        rows[slot * count : (slot + 1) * count, :] = gathered[slot]
+
+    def group_sum(value, stage, mine, peer):
+        box = grams.at[stage]
+        box[mine] = value
+        for k in range(1, GROUP):
+            copy = send(
+                box.at[mine], box.at[mine], gram_send.at[stage, k], gram_recv.at[stage, mine],
+                peer(k),
+            )
+            copy.start()
+            copies.append(copy)
+        for k in range(1, GROUP):
+            slot = lax.rem(mine + k, GROUP)
+            send(
+                box.at[slot], box.at[slot], gram_send.at[stage, k], gram_recv.at[stage, slot],
+                peer(k),
+            ).wait_recv()
+        total = box[0]
+        for slot in range(1, GROUP):
+            total = total + box[slot]
+        return total
+
+    def space_gram(basis, stage):
+        gram = dot_highest(basis, basis, ((1,), (1,)))
+        gram = group_sum(gram, stage, inner, inner_peer)
+        gram = group_sum(gram, stage + 1, outer, outer_peer)
+        return gram * (1.0 / cell_count)
+
+    images = rows[...]
+    factor_one, inverse_one = factor_and_inverse(space_gram(images, 0))
+    basis_one = dot_highest(inverse_one, images, ((1,), (0,)))
+    factor_two, inverse_two = factor_and_inverse(space_gram(basis_one, 2))
+    q_rows = dot_highest(inverse_two, basis_one, ((1,), (0,)))
+    for slot in range(GROUP):
+        gathered[slot] = q_rows[slot * count : (slot + 1) * count, :]
+    q_ref[...] = gathered[me]
+    lower_ref[...] = dot_highest(factor_one, factor_two, ((1,), (0,)))
+    for copy in copies:
+        copy.wait_send()
+
+
+def orthogonalize(images, cell_count):
+    count, cells = images.shape
+    probes = count * GROUP
+    vmem = pl.BlockSpec(memory_space=pltpu.VMEM)
+
+    def body(*refs):
+        orthogonalize_kernel(cell_count, *refs)
+
+    return pl.pallas_call(
+        body,
+        out_shape=(
+            jax.ShapeDtypeStruct((count, cells), jnp.float32),
+            jax.ShapeDtypeStruct((probes, probes), jnp.float32),
+        ),
+        in_specs=[vmem],
+        out_specs=(vmem, vmem),
+        scratch_shapes=[
+            pltpu.VMEM((GROUP, count, cells), jnp.float32),
+            pltpu.VMEM((probes, cells), jnp.float32),
+            pltpu.VMEM((4, GROUP, probes, probes), jnp.float32),
+            pltpu.SemaphoreType.DMA((GROUP,)),
+            pltpu.SemaphoreType.DMA((GROUP,)),
+            pltpu.SemaphoreType.DMA((4, GROUP)),
+            pltpu.SemaphoreType.DMA((4, GROUP)),
+        ],
+        compiler_params=pltpu.CompilerParams(collective_id=0, has_side_effects=True),
+    )(images)
 
 
 def shards(probe_dirs, log_param, background, site_class, trap_density):
@@ -87,20 +224,7 @@
         summed = summed + adjoint
     images = restrict(source[None] * summed).reshape((probe_count, planes * plane_cells))
     cell_count = float(planes * lax.axis_size("space") * plane_cells)
-    highest = lax.Precision.HIGHEST
-    every_probe = lax.all_gather(images, "probe", axis=0, tiled=True)
-
-    def space_sum(partial_gram):
-        return lax.psum(partial_gram, "space")
-
-    basis_one, factor_one = cholesky_pass(every_probe, space_sum, cell_count)
-    q_rows, factor_two = cholesky_pass(basis_one, space_sum, cell_count)
-    q_local = lax.dynamic_slice_in_dim(
-        q_rows, lax.axis_index("probe") * probe_count, probe_count, 0
-    )
-    lower_factor = jnp.dot(
-        factor_one, factor_two, precision=highest, preferred_element_type=jnp.float32
-    )
+    q_local, lower_factor = orthogonalize(images, cell_count)
     return (q_local.reshape((probe_count, planes, plane_cells)), lower_factor)
 
 

time: 1070 us -> 218 us (0.20)
  the two profiles are of different devices: /device:TPU:56 before, /device:TPU:6 now
where the time goes in v2:
time: 218 us; the launch traced here: 216 us
  Pallas kernels  89.8 us (41%)
  starting transfers between devices  42.5 us (19%)
  waiting for transfers between devices  42.4 us (19%)
  other arithmetic  23.8 us (11%)
  local copies, waits for them, and re-layouts  16.8 us (8%)
    pallas_call x1, Pallas kernels, orthogonalize(): pl.pallas_call(body, out_shape=(jax.ShapeDtypeStruct((count, cells), jnp....  89.8 us
    ppermute x6, waiting for transfers between devices, padded_2(): before = lax.ppermute(last, axis, up)  26.4 us
    ppermute x6, starting transfers between devices, padded_2(): before = lax.ppermute(last, axis, up)  21.7 us
    ppermute x6, starting transfers between devices, padded_2(): after = lax.ppermute(first, axis, down)  20.8 us
    ppermute x6, waiting for transfers between devices, padded_2(): after = lax.ppermute(first, axis, down)  16 us
    add x5, other arithmetic, stencil(): current + TIME_STEP * (up_down + lateral - 6.0 * current - trap_rate[None...  12.2 us
    reduce_sum x2, other arithmetic, restrict(): jnp.sum(shaped, axis=(2, 4, 6)).reshape((probe_count, planes, PY * PX))  7.79 us
    broadcast_in_dim x4, local copies, waits for them, and re-layouts, prolong(): jnp.broadcast_to(coarse_grid[..., :, None, :, None, :, None], leading + (...  6.87 us
  transfers between devices with their start and end apart: 12, of which 12 were waited for; matrix products, arithmetic and copies ran while one was open for 0% of the time, Pallas kernels for 0%

profile of v2, /device:TPU:6, one launch (start us, length us, event | category | flops | bytes accessed | tf_op | source)
XLA Modules:
  0.0 216.1 jit_solution(1039753943203246876)
XLA Ops:
  4.4 2.5 %broadcast_in_dim.54 = f32[4,4,8,64,8]{4,3,2,1,0:T(8,128)} broadcast(f32[4,4,64]{2,1,0:T(4,128)S(1)} %broadcast_in_dim.53), dimensions={0,1,3} | broadcast | bytes 266240 | tf_op jit(solution)/shard_map/broadcast_in_dim | solution.py:34
  6.9 4.1 %broadcast_in_dim.55 = f32[4,32,512]{2,1,0:T(8,128)S(1)} reshape(f32[4,4,8,64,8]{4,3,2,1,0:T(8,128)} %broadcast_in_dim.54) | data formatting | bytes 524288 | tf_op jit(solution)/shard_map/broadcast_in_dim | solution.py:34
  11.0 2.8 %multiply_multiply_fusion.2 = (f32[8,32,512]{2,1,0:T(8,128)S(1)}, f32[8,32,512]{2,1,0:T(8,128)S(1)}) fusion(f32[8,32,512]{2,1,0:T(8,128)S(1)} %copy-done, f32[32,512]{1,0:T(8,128)S(1)} %exp.13, f32[]{:T(128)} %bitcast.3, s32[8,32,512]{2,1,0:T(8,128)S(1)} %copy-done.1, f32[]{:T(128)} %bitcast.2, f32[]{:T(128)} %bitcast.1, f32[]{:T(128)} %bitcast), kind=kLoop, calls=%fused_computation.96 | loop fusion | flops 1835008 | bytes 2162704 | tf_op jit(solution)/shard_map/mul | solution.py:214
  14.1 11.2 %collective-permute-start = (f32[4,1,32,512]{3,2,1,0:T(8,128)S(1)}, f32[4,1,32,512]{3,2,1,0:T(8,128)S(1)}, u32[]{:S(2)}, u32[]{:S(2)}) collective-permute-start(f32[4,1,32,512]{3,2,1,0:T(8,128)S(1)} %get-tuple-element.24), channel_id=1, source_target_pairs={{1,0},{2,1},{3,2},{4,3},{5,4},{6,5},{7,6},{8,7},{9,8},{10,9},{11,1... | collective-permute-start | bytes 786440 | tf_op jit(solution)/shard_map/ppermute | solution.py:25
  25.4 1.9 collective-permute-start.1
  27.3 3.6 %collective-permute-done = f32[4,1,32,512]{3,2,1,0:T(8,128)S(1)} collective-permute-done((f32[4,1,32,512]{3,2,1,0:T(8,128)S(1)}, f32[4,1,32,512]{3,2,1,0:T(8,128)S(1)}, u32[]{:S(2)}, u32[]{:S(2)}) %collective-permute-start) | collective-permute-done | bytes 262176 | tf_op jit(solution)/shard_map/ppermute | solution.py:25
  30.9 6.2 %collective-permute-done.1 = f32[4,1,32,512]{3,2,1,0:T(8,128)S(1)} collective-permute-done((f32[4,1,32,512]{3,2,1,0:T(8,128)S(1)}, f32[4,1,32,512]{3,2,1,0:T(8,128)S(1)}, u32[]{:S(2)}, u32[]{:S(2)}) %collective-permute-start.1) | collective-permute-done | bytes 262176 | tf_op jit(solution)/shard_map/ppermute | solution.py:24
  37.1 2.4 %multiply_add_fusion = f32[4,8,32,512]{3,2,1,0:T(8,128)S(1)} fusion(f32[4,8,32,512]{3,2,1,0:T(8,128)S(1)} %broadcast_multiply_fusion, f32[4,1,32,512]{3,2,1,0:T(8,128)S(1)} %collective-permute-done.1, f32[4,1,32,512]{3,2,1,0:T(8,128)S(1)} %collective-permute-done, f32[8,32,512]{2,1,0:T(8,128)S(1)} %get-tuple-element.13, ...), kind=kLoop, calls=%fused_computation.24 | loop fusion | flops 7340032 | bytes 6029312 | tf_op jit(solution)/shard_map/add | solution.py:56
  41.5 3.9 %collective-permute-start.3 = (f32[4,1,32,512]{3,2,1,0:T(8,128)S(1)}, f32[4,1,32,512]{3,2,1,0:T(8,128)S(1)}, u32[]{:S(2)}, u32[]{:S(2)}) collective-permute-start(f32[4,1,32,512]{3,2,1,0:T(8,128)S(1)} %get-tuple-element.23), channel_id=1, source_target_pairs={{0,1},{1,2},{2,3},{3,4},{4,5},{5,6},{6,7},{7,8},{8,9},{9,10},{10,1... | collective-permute-start | bytes 786440 | tf_op jit(solution)/shard_map/ppermute | solution.py:24
  45.4 2.9 %collective-permute-done.2 = f32[4,1,32,512]{3,2,1,0:T(8,128)S(1)} collective-permute-done((f32[4,1,32,512]{3,2,1,0:T(8,128)S(1)}, f32[4,1,32,512]{3,2,1,0:T(8,128)S(1)}, u32[]{:S(2)}, u32[]{:S(2)}) %collective-permute-start.2) | collective-permute-done | bytes 262176 | tf_op jit(solution)/shard_map/ppermute | solution.py:25
  48.4 4.0 %collective-permute-done.3 = f32[4,1,32,512]{3,2,1,0:T(8,128)S(1)} collective-permute-done((f32[4,1,32,512]{3,2,1,0:T(8,128)S(1)}, f32[4,1,32,512]{3,2,1,0:T(8,128)S(1)}, u32[]{:S(2)}, u32[]{:S(2)}) %collective-permute-start.3) | collective-permute-done | bytes 262176 | tf_op jit(solution)/shard_map/ppermute | solution.py:24
  52.4 2.5 %fusion.14 = f32[4,8,32,512]{3,2,1,0:T(8,128)S(1)} fusion(f32[4,8,32,512]{3,2,1,0:T(8,128)S(1)} %multiply_add_fusion, f32[4,1,32,512]{3,2,1,0:T(8,128)S(1)} %collective-permute-done.3, f32[4,1,32,512]{3,2,1,0:T(8,128)S(1)} %collective-permute-done.2, f32[8,32,512]{2,1,0:T(8,128)S(1)} %get-tuple-element.13), kind=kLoop, calls=%fused_computation.41 | loop fusion | flops 6815744 | bytes 5242880 | tf_op jit(solution)/shard_map/add | solution.py:56
  55.0 1.9 collective-permute-start.4
  56.9 3.9 %collective-permute-start.5 = (f32[4,1,32,512]{3,2,1,0:T(8,128)S(1)}, f32[4,1,32,512]{3,2,1,0:T(8,128)S(1)}, u32[]{:S(2)}, u32[]{:S(2)}) collective-permute-start(f32[4,1,32,512]{3,2,1,0:T(8,128)S(1)} %get-tuple-element.21), channel_id=1, source_target_pairs={{0,1},{1,2},{2,3},{3,4},{4,5},{5,6},{6,7},{7,8},{8,9},{9,10},{10,1... | collective-permute-start | bytes 786440 | tf_op jit(solution)/shard_map/ppermute | solution.py:24
  60.8 2.4 %collective-permute-done.4 = f32[4,1,32,512]{3,2,1,0:T(8,128)S(1)} collective-permute-done((f32[4,1,32,512]{3,2,1,0:T(8,128)S(1)}, f32[4,1,32,512]{3,2,1,0:T(8,128)S(1)}, u32[]{:S(2)}, u32[]{:S(2)}) %collective-permute-start.4) | collective-permute-done | bytes 262176 | tf_op jit(solution)/shard_map/ppermute | solution.py:25
  63.2 4.0 %collective-permute-done.5 = f32[4,1,32,512]{3,2,1,0:T(8,128)S(1)} collective-permute-done((f32[4,1,32,512]{3,2,1,0:T(8,128)S(1)}, f32[4,1,32,512]{3,2,1,0:T(8,128)S(1)}, u32[]{:S(2)}, u32[]{:S(2)}) %collective-permute-start.5) | collective-permute-done | bytes 262176 | tf_op jit(solution)/shard_map/ppermute | solution.py:24
  67.3 2.5 %fusion.22 = f32[4,8,32,512]{3,2,1,0:T(8,128)S(1)} fusion(f32[4,8,32,512]{3,2,1,0:T(8,128)S(1)} %fusion.14, f32[4,1,32,512]{3,2,1,0:T(8,128)S(1)} %collective-permute-done.5, f32[4,1,32,512]{3,2,1,0:T(8,128)S(1)} %collective-permute-done.4, f32[8,32,512]{2,1,0:T(8,128)S(1)} %get-tuple-element.13), kind=kLoop, calls=%fused_computation.49 | loop fusion | flops 6815744 | bytes 5242880 | tf_op jit(solution)/shard_map/add | solution.py:56
  71.7 3.9 %collective-permute-start.7 = (f32[4,1,32,512]{3,2,1,0:T(8,128)S(1)}, f32[4,1,32,512]{3,2,1,0:T(8,128)S(1)}, u32[]{:S(2)}, u32[]{:S(2)}) collective-permute-start(f32[4,1,32,512]{3,2,1,0:T(8,128)S(1)} %get-tuple-element.19), channel_id=1, source_target_pairs={{0,1},{1,2},{2,3},{3,4},{4,5},{5,6},{6,7},{7,8},{8,9},{9,10},{10,1... | collective-permute-start | bytes 786440 | tf_op jit(solution)/shard_map/ppermute | solution.py:24
  75.7 2.4 %collective-permute-done.6 = f32[4,1,32,512]{3,2,1,0:T(8,128)S(1)} collective-permute-done((f32[4,1,32,512]{3,2,1,0:T(8,128)S(1)}, f32[4,1,32,512]{3,2,1,0:T(8,128)S(1)}, u32[]{:S(2)}, u32[]{:S(2)}) %collective-permute-start.6) | collective-permute-done | bytes 262176 | tf_op jit(solution)/shard_map/ppermute | solution.py:25
  78.1 4.0 %collective-permute-done.7 = f32[4,1,32,512]{3,2,1,0:T(8,128)S(1)} collective-permute-done((f32[4,1,32,512]{3,2,1,0:T(8,128)S(1)}, f32[4,1,32,512]{3,2,1,0:T(8,128)S(1)}, u32[]{:S(2)}, u32[]{:S(2)}) %collective-permute-start.7) | collective-permute-done | bytes 262176 | tf_op jit(solution)/shard_map/ppermute | solution.py:24
  82.1 2.3 %fusion.30 = f32[4,8,32,512]{3,2,1,0:T(8,128)S(1)} fusion(f32[4,8,32,512]{3,2,1,0:T(8,128)S(1)} %fusion.22, f32[4,1,32,512]{3,2,1,0:T(8,128)S(1)} %collective-permute-done.7, f32[4,1,32,512]{3,2,1,0:T(8,128)S(1)} %collective-permute-done.6, f32[8,32,512]{2,1,0:T(8,128)S(1)} %get-tuple-element.13), kind=kLoop, calls=%fused_computation.57 | loop fusion | flops 6815744 | bytes 5242880 | tf_op jit(solution)/shard_map/add | solution.py:56
  86.4 3.9 %collective-permute-start.9 = (f32[4,1,32,512]{3,2,1,0:T(8,128)S(1)}, f32[4,1,32,512]{3,2,1,0:T(8,128)S(1)}, u32[]{:S(2)}, u32[]{:S(2)}) collective-permute-start(f32[4,1,32,512]{3,2,1,0:T(8,128)S(1)} %get-tuple-element.17), channel_id=1, source_target_pairs={{0,1},{1,2},{2,3},{3,4},{4,5},{5,6},{6,7},{7,8},{8,9},{9,10},{10,1... | collective-permute-start | bytes 786440 | tf_op jit(solution)/shard_map/ppermute | solution.py:24
  90.4 2.4 %collective-permute-done.8 = f32[4,1,32,512]{3,2,1,0:T(8,128)S(1)} collective-permute-done((f32[4,1,32,512]{3,2,1,0:T(8,128)S(1)}, f32[4,1,32,512]{3,2,1,0:T(8,128)S(1)}, u32[]{:S(2)}, u32[]{:S(2)}) %collective-permute-start.8) | collective-permute-done | bytes 262176 | tf_op jit(solution)/shard_map/ppermute | solution.py:25
  92.8 4.0 %collective-permute-done.9 = f32[4,1,32,512]{3,2,1,0:T(8,128)S(1)} collective-permute-done((f32[4,1,32,512]{3,2,1,0:T(8,128)S(1)}, f32[4,1,32,512]{3,2,1,0:T(8,128)S(1)}, u32[]{:S(2)}, u32[]{:S(2)}) %collective-permute-start.9) | collective-permute-done | bytes 262176 | tf_op jit(solution)/shard_map/ppermute | solution.py:24
  96.8 2.5 %fusion.38 = f32[4,8,32,512]{3,2,1,0:T(8,128)S(1)} fusion(f32[4,8,32,512]{3,2,1,0:T(8,128)S(1)} %fusion.30, f32[4,1,32,512]{3,2,1,0:T(8,128)S(1)} %collective-permute-done.9, f32[4,1,32,512]{3,2,1,0:T(8,128)S(1)} %collective-permute-done.8, f32[8,32,512]{2,1,0:T(8,128)S(1)} %get-tuple-element.13), kind=kLoop, calls=%fused_computation.65 | loop fusion | flops 6815744 | bytes 5242880 | tf_op jit(solution)/shard_map/add | solution.py:56
  101.3 4.1 %collective-permute-start.11 = (f32[4,1,32,512]{3,2,1,0:T(8,128)S(1)}, f32[4,1,32,512]{3,2,1,0:T(8,128)S(1)}, u32[]{:S(2)}, u32[]{:S(2)}) collective-permute-start(f32[4,1,32,512]{3,2,1,0:T(8,128)S(1)} %get-tuple-element.15), channel_id=1, source_target_pairs={{0,1},{1,2},{2,3},{3,4},{4,5},{5,6},{6,7},{7,8},{8,9},{9,10},{10,1... | collective-permute-start | bytes 786440 | tf_op jit(solution)/shard_map/ppermute | solution.py:24
  105.4 2.2 %collective-permute-done.10 = f32[4,1,32,512]{3,2,1,0:T(8,128)S(1)} collective-permute-done((f32[4,1,32,512]{3,2,1,0:T(8,128)S(1)}, f32[4,1,32,512]{3,2,1,0:T(8,128)S(1)}, u32[]{:S(2)}, u32[]{:S(2)}) %collective-permute-start.10) | collective-permute-done | bytes 262176 | tf_op jit(solution)/shard_map/ppermute | solution.py:25
  107.6 4.0 %collective-permute-done.11 = f32[4,1,32,512]{3,2,1,0:T(8,128)S(1)} collective-permute-done((f32[4,1,32,512]{3,2,1,0:T(8,128)S(1)}, f32[4,1,32,512]{3,2,1,0:T(8,128)S(1)}, u32[]{:S(2)}, u32[]{:S(2)}) %collective-permute-start.11) | collective-permute-done | bytes 262176 | tf_op jit(solution)/shard_map/ppermute | solution.py:24
  111.7 5.2 %fusion.55 = f32[4,32,512]{2,1,0:T(8,128)S(1)} fusion(f32[4,8,32,512]{3,2,1,0:T(8,128)S(1)} %fusion.38, f32[4,1,32,512]{3,2,1,0:T(8,128)S(1)} %collective-permute-done.11, f32[4,1,32,512]{3,2,1,0:T(8,128)S(1)} %collective-permute-done.10, f32[4,8,32,512]{3,2,1,0:T(8,128)S(1)} %fusion.22, f32[8,32,512]{2,1,0:T(8,128)S(1)} %get-tuple-element.13, ...), kind=kLoop, calls=%fused_computation.94 | loop fusion | flops 16187392 | bytes 6553600 | tf_op jit(solution)/shard_map/reduce_sum | solution.py:44
  116.9 3.6 %reduce_sum.14 = f32[4,4,8,64,8]{4,3,2,1,0:T(8,128)} reshape(f32[4,32,512]{2,1,0:T(8,128)S(1)} %fusion.55) | data formatting | bytes 524288 | tf_op jit(solution)/shard_map/reduce_sum | solution.py:44
  120.5 2.6 %reduce_sum.18 = f32[4,4,64]{2,1,0:T(4,128)S(1)} reduce(f32[4,4,8,64,8]{4,3,2,1,0:T(8,128)} %reduce_sum.14, f32[]{:T(128)} %constant.1.clone.1), dimensions={2,4}, to_apply=%region_1.2 | reduce | flops 64512 | bytes 266244 | tf_op jit(solution)/shard_map/reduce_sum | solution.py:44
  123.8 89.8 %shard_map.68 = (f32[4,256]{1,0:T(4,128)}, f32[32,32]{1,0:T(8,128)}) custom-call(f32[4,256]{1,0:T(4,128)} %reshape_reshape.3.refs_0_), custom_call_target="tpu_custom_call" | custom-call | tf_op jit(solution)/shard_map/pallas_call | solution.py:185
  (25 shorter events, 15.2 us)
Async XLA Ops:
  6.9 4.1 %copy-start = (f32[8,32,512]{2,1,0:T(8,128)S(1)}, f32[8,32,512]{2,1,0:T(8,128)}, u32[]{:S(2)}) copy-start(f32[8,32,512]{2,1,0:T(8,128)} %param.7) | copy-start | bytes 1572868
  6.9 4.1 %copy-start.1 = (s32[8,32,512]{2,1,0:T(8,128)S(1)}, s32[8,32,512]{2,1,0:T(8,128)}, u32[]{:S(2)}) copy-start(s32[8,32,512]{2,1,0:T(8,128)} %param.8) | copy-start | bytes 1572868
  14.1 16.8 %collective-permute-start = (f32[4,1,32,512]{3,2,1,0:T(8,128)S(1)}, f32[4,1,32,512]{3,2,1,0:T(8,128)S(1)}, u32[]{:S(2)}, u32[]{:S(2)}) collective-permute-start(f32[4,1,32,512]{3,2,1,0:T(8,128)S(1)} %get-tuple-element.24), channel_id=1, source_target_pairs={{1,0},{2,1},{3,2},{4,3},{5,4},{6,5},{7,6},{8,7},{9,8},{10,9},{11,1... | collective-permute-start | bytes 786440 | tf_op jit(solution)/shard_map/ppermute | solution.py:25
  25.4 11.8 %collective-permute-start.1 = (f32[4,1,32,512]{3,2,1,0:T(8,128)S(1)}, f32[4,1,32,512]{3,2,1,0:T(8,128)S(1)}, u32[]{:S(2)}, u32[]{:S(2)}) collective-permute-start(f32[4,1,32,512]{3,2,1,0:T(8,128)S(1)} %get-tuple-element.25), channel_id=1, source_target_pairs={{0,1},{1,2},{2,3},{3,4},{4,5},{5,6},{6,7},{7,8},{8,9},{9,10},{10,1... | collective-permute-start | bytes 786440 | tf_op jit(solution)/shard_map/ppermute | solution.py:24
  39.6 8.8 %collective-permute-start.2 = (f32[4,1,32,512]{3,2,1,0:T(8,128)S(1)}, f32[4,1,32,512]{3,2,1,0:T(8,128)S(1)}, u32[]{:S(2)}, u32[]{:S(2)}) collective-permute-start(f32[4,1,32,512]{3,2,1,0:T(8,128)S(1)} %get-tuple-element.22), channel_id=1, source_target_pairs={{1,0},{2,1},{3,2},{4,3},{5,4},{6,5},{7,6},{8,7},{9,8},{10,9},{11,1... | collective-permute-start | bytes 786440 | tf_op jit(solution)/shard_map/ppermute | solution.py:25
  41.5 10.9 %collective-permute-start.3 = (f32[4,1,32,512]{3,2,1,0:T(8,128)S(1)}, f32[4,1,32,512]{3,2,1,0:T(8,128)S(1)}, u32[]{:S(2)}, u32[]{:S(2)}) collective-permute-start(f32[4,1,32,512]{3,2,1,0:T(8,128)S(1)} %get-tuple-element.23), channel_id=1, source_target_pairs={{0,1},{1,2},{2,3},{3,4},{4,5},{5,6},{6,7},{7,8},{8,9},{9,10},{10,1... | collective-permute-start | bytes 786440 | tf_op jit(solution)/shard_map/ppermute | solution.py:24
  55.0 8.3 %collective-permute-start.4 = (f32[4,1,32,512]{3,2,1,0:T(8,128)S(1)}, f32[4,1,32,512]{3,2,1,0:T(8,128)S(1)}, u32[]{:S(2)}, u32[]{:S(2)}) collective-permute-start(f32[4,1,32,512]{3,2,1,0:T(8,128)S(1)} %get-tuple-element.20), channel_id=1, source_target_pairs={{1,0},{2,1},{3,2},{4,3},{5,4},{6,5},{7,6},{8,7},{9,8},{10,9},{11,1... | collective-permute-start | bytes 786440 | tf_op jit(solution)/shard_map/ppermute | solution.py:25
  56.9 10.4 %collective-permute-start.5 = (f32[4,1,32,512]{3,2,1,0:T(8,128)S(1)}, f32[4,1,32,512]{3,2,1,0:T(8,128)S(1)}, u32[]{:S(2)}, u32[]{:S(2)}) collective-permute-start(f32[4,1,32,512]{3,2,1,0:T(8,128)S(1)} %get-tuple-element.21), channel_id=1, source_target_pairs={{0,1},{1,2},{2,3},{3,4},{4,5},{5,6},{6,7},{7,8},{8,9},{9,10},{10,1... | collective-permute-start | bytes 786440 | tf_op jit(solution)/shard_map/ppermute | solution.py:24
  69.8 8.3 %collective-permute-start.6 = (f32[4,1,32,512]{3,2,1,0:T(8,128)S(1)}, f32[4,1,32,512]{3,2,1,0:T(8,128)S(1)}, u32[]{:S(2)}, u32[]{:S(2)}) collective-permute-start(f32[4,1,32,512]{3,2,1,0:T(8,128)S(1)} %get-tuple-element.18), channel_id=1, source_target_pairs={{1,0},{2,1},{3,2},{4,3},{5,4},{6,5},{7,6},{8,7},{9,8},{10,9},{11,1... | collective-permute-start | bytes 786440 | tf_op jit(solution)/shard_map/ppermute | solution.py:25
  71.7 10.4 %collective-permute-start.7 = (f32[4,1,32,512]{3,2,1,0:T(8,128)S(1)}, f32[4,1,32,512]{3,2,1,0:T(8,128)S(1)}, u32[]{:S(2)}, u32[]{:S(2)}) collective-permute-start(f32[4,1,32,512]{3,2,1,0:T(8,128)S(1)} %get-tuple-element.19), channel_id=1, source_target_pairs={{0,1},{1,2},{2,3},{3,4},{4,5},{5,6},{6,7},{7,8},{8,9},{9,10},{10,1... | collective-permute-start | bytes 786440 | tf_op jit(solution)/shard_map/ppermute | solution.py:24
  84.5 8.3 %collective-permute-start.8 = (f32[4,1,32,512]{3,2,1,0:T(8,128)S(1)}, f32[4,1,32,512]{3,2,1,0:T(8,128)S(1)}, u32[]{:S(2)}, u32[]{:S(2)}) collective-permute-start(f32[4,1,32,512]{3,2,1,0:T(8,128)S(1)} %get-tuple-element.16), channel_id=1, source_target_pairs={{1,0},{2,1},{3,2},{4,3},{5,4},{6,5},{7,6},{8,7},{9,8},{10,9},{11,1... | collective-permute-start | bytes 786440 | tf_op jit(solution)/shard_map/ppermute | solution.py:25
  86.4 10.4 %collective-permute-start.9 = (f32[4,1,32,512]{3,2,1,0:T(8,128)S(1)}, f32[4,1,32,512]{3,2,1,0:T(8,128)S(1)}, u32[]{:S(2)}, u32[]{:S(2)}) collective-permute-start(f32[4,1,32,512]{3,2,1,0:T(8,128)S(1)} %get-tuple-element.17), channel_id=1, source_target_pairs={{0,1},{1,2},{2,3},{3,4},{4,5},{5,6},{6,7},{7,8},{8,9},{9,10},{10,1... | collective-permute-start | bytes 786440 | tf_op jit(solution)/shard_map/ppermute | solution.py:24
  99.3 8.3 %collective-permute-start.10 = (f32[4,1,32,512]{3,2,1,0:T(8,128)S(1)}, f32[4,1,32,512]{3,2,1,0:T(8,128)S(1)}, u32[]{:S(2)}, u32[]{:S(2)}) collective-permute-start(f32[4,1,32,512]{3,2,1,0:T(8,128)S(1)} %get-tuple-element.14), channel_id=1, source_target_pairs={{1,0},{2,1},{3,2},{4,3},{5,4},{6,5},{7,6},{8,7},{9,8},{10,9},{11,1... | collective-permute-start | bytes 786440 | tf_op jit(solution)/shard_map/ppermute | solution.py:25
  101.3 10.4 %collective-permute-start.11 = (f32[4,1,32,512]{3,2,1,0:T(8,128)S(1)}, f32[4,1,32,512]{3,2,1,0:T(8,128)S(1)}, u32[]{:S(2)}, u32[]{:S(2)}) collective-permute-start(f32[4,1,32,512]{3,2,1,0:T(8,128)S(1)} %get-tuple-element.15), channel_id=1, source_target_pairs={{0,1},{1,2},{2,3},{3,4},{4,5},{5,6},{6,7},{7,8},{8,9},{9,10},{10,1... | collective-permute-start | bytes 786440 | tf_op jit(solution)/shard_map/ppermute | solution.py:24

commit v3 on v2

--- a/solution.py
+++ b/solution.py
@@ -12,19 +12,6 @@
 
 
 TIME_STEP = 0.12
-
-
-def padded_2(x, sides, width):
-    for axis, dim in sides:
-        count, length = (lax.axis_size(axis), x.shape[dim])
-        up = [(i, (i + 1) % count) for i in range(count - 1)]
-        down = [(j, i) for i, j in up]
-        last = lax.slice_in_dim(x, length - width, length, axis=dim)
-        first = lax.slice_in_dim(x, 0, width, axis=dim)
-        before = lax.ppermute(last, axis, up)
-        after = lax.ppermute(first, axis, down)
-        x = jnp.concatenate([before, x, after], axis=dim)
-    return x
 
 
 def prolong(coarse):
@@ -35,25 +22,6 @@
         coarse_grid[..., :, None, :, None, :, None], leading + (planes, REF, PY, REF, PX, REF)
     )
     return expanded.reshape(leading + (planes * REF, PY * REF, PX * REF))
-
-
-def restrict(finegrid):
-    probe_count = finegrid.shape[0]
-    planes = finegrid.shape[1] // REF
-    shaped = finegrid.reshape((probe_count, planes, REF, PY, REF, PX, REF))
-    return jnp.sum(shaped, axis=(2, 4, 6)).reshape((probe_count, planes, PY * PX))
-
-
-def stencil(padded, current, trap_rate):
-    up_down = padded[:, 2:, :, :] + padded[:, :-2, :, :]
-    flat_pad = jnp.pad(current, ((0, 0), (0, 0), (1, 1), (1, 1)))
-    lateral = (
-        flat_pad[:, :, 2:, 1:-1]
-        + flat_pad[:, :, :-2, 1:-1]
-        + flat_pad[:, :, 1:-1, 2:]
-        + flat_pad[:, :, 1:-1, :-2]
-    )
-    return current + TIME_STEP * (up_down + lateral - 6.0 * current - trap_rate[None] * current)
 
 
 def dot_highest(a, b, contract):
@@ -203,27 +171,146 @@
     )(images)
 
 
+REACH = 2 * (STEPS - 1)
+EXTENDED = REF + 2 * REACH
+CHUNK = 16
+
+
+def window_kernel(
+    edge_ref, trap_ref, source_ref, halo_ref, dirs_ref, images_ref, keep, source, first, second,
+    summed,
+):
+    fine_y, fine_x = PY * REF, PX * REF
+    share = halo_ref.shape[2] // CHUNK
+    own = slice(REACH, REACH + REF)
+    keep[own] = (1.0 - 6.0 * TIME_STEP) - TIME_STEP * trap_ref[...]
+    source[own] = source_ref[...]
+    for side in range(2):
+        base = side * (REACH + REF)
+        inside = edge_ref[side]
+        for plane in range(REACH):
+            for half in range(fine_y // CHUNK):
+                rows = slice(half * CHUNK, (half + 1) * CHUNK)
+
+                def piece(at):
+                    chunk = at * (fine_y // CHUNK) + half
+                    start = (chunk % share) * CHUNK
+                    return halo_ref[chunk // share, side, start : start + CHUNK, :]
+
+                trap = piece(plane)
+                keep[base + plane, rows, :] = inside * (
+                    (1.0 - 6.0 * TIME_STEP) - TIME_STEP * trap
+                )
+                source[base + plane, rows, :] = inside * piece(REACH + plane)
+
+    x_fine = lax.broadcasted_iota(jnp.int32, (PX, fine_x), 1)
+    x_cell = lax.broadcasted_iota(jnp.int32, (PX, fine_x), 0)
+    spread_x = jnp.where(x_fine // REF == x_cell, 1.0, 0.0)
+    y_fine = lax.broadcasted_iota(jnp.int32, (fine_y, PY), 0)
+    y_cell = lax.broadcasted_iota(jnp.int32, (fine_y, PY), 1)
+    spread_y = jnp.where(y_fine // REF == y_cell, 1.0, 0.0)
+    row_at = lax.broadcasted_iota(jnp.int32, (fine_y, fine_x), 0)
+    lane_at = lax.broadcasted_iota(jnp.int32, (fine_y, fine_x), 1)
+
+    def advance(src, dst, low, high, add):
+        def plane_step(i, carry):
+            below = (i >= REACH).astype(jnp.float32)
+            above = (i < REACH + REF).astype(jnp.float32)
+            weight = TIME_STEP * (below + (1.0 - below) * edge_ref[0])
+            weight = weight * (above + (1.0 - above) * edge_ref[1])
+            v = src[i]
+            around = src[i - 1] + src[i + 1]
+            around += jnp.where(row_at == 0, 0.0, pltpu.roll(v, 1, 0))
+            around += jnp.where(row_at == fine_y - 1, 0.0, pltpu.roll(v, fine_y - 1, 0))
+            around += jnp.where(lane_at == 0, 0.0, pltpu.roll(v, 1, 1))
+            around += jnp.where(lane_at == fine_x - 1, 0.0, pltpu.roll(v, fine_x - 1, 1))
+            new = keep[i] * v + weight * around
+            dst[i] = new
+            if add:
+                @pl.when((i >= REACH) & (i < REACH + REF))
+                def _():
+                    at = i - REACH
+                    summed[at] = summed[at] + new
+            return carry
+
+        lax.fori_loop(low, high, plane_step, 0)
+
+    def probe_step(p, carry):
+        for cell in range(3):
+            coarse = dirs_ref[p, cell]
+            wide = dot_highest(coarse, spread_x, ((1,), (0,)))
+            fine = dot_highest(spread_y, wide, ((1,), (0,)))
+            low = max(0, REACH - REF + cell * REF)
+            high = min(EXTENDED, REACH + cell * REF)
+            for i in range(low, high):
+                first[i] = source[i] * fine
+        bufs = (first, second)
+        for n in range(1, 2 * STEPS - 1):
+            src, dst = bufs[(n - 1) % 2], bufs[n % 2]
+            advance(src, dst, n, EXTENDED - n, n >= STEPS)
+            if n == STEPS - 1:
+                summed[...] = dst[own]
+        total = source[REACH] * summed[0]
+        for at in range(1, REF):
+            total = total + source[REACH + at] * summed[at]
+        narrow = dot_highest(total, spread_x, ((1,), (1,)))
+        images_ref[p] = dot_highest(spread_y, narrow, ((0,), (0,)))
+        return carry
+
+    lax.fori_loop(0, dirs_ref.shape[0], probe_step, 0)
+
+
+def window_images(edge, trap_rate, source, halo, dirs):
+    vmem = pl.BlockSpec(memory_space=pltpu.VMEM)
+    plane = (PY * REF, PX * REF)
+    return pl.pallas_call(
+        window_kernel,
+        out_shape=jax.ShapeDtypeStruct((dirs.shape[0], PY, PX), jnp.float32),
+        in_specs=[pl.BlockSpec(memory_space=pltpu.SMEM)] + [vmem] * 4,
+        out_specs=vmem,
+        scratch_shapes=[
+            pltpu.VMEM((EXTENDED,) + plane, jnp.float32),
+            pltpu.VMEM((EXTENDED,) + plane, jnp.float32),
+            pltpu.VMEM((EXTENDED,) + plane, jnp.float32),
+            pltpu.VMEM((EXTENDED,) + plane, jnp.float32),
+            pltpu.VMEM((REF,) + plane, jnp.float32),
+        ],
+        compiler_params=pltpu.CompilerParams(vmem_limit_bytes=32 * 1024 * 1024),
+    )(edge, trap_rate, source, halo, dirs)
+
+
 def shards(probe_dirs, log_param, background, site_class, trap_density):
-    probe_count = probe_dirs.shape[0]
-    planes = probe_dirs.shape[1]
-    plane_cells = probe_dirs.shape[2]
+    probe_count, planes, plane_cells = probe_dirs.shape
+    slabs, slab = lax.axis_size("space"), lax.axis_index("space")
+    up = [(i, i + 1) for i in range(slabs - 1)]
+    down = [(j, i) for i, j in up]
     density = jnp.zeros(site_class.shape, jnp.float32)
     for class_index in range(trap_density.shape[0]):
         density = density + jnp.where(site_class == class_index, trap_density[class_index], 0.0)
-    trap_rate = density * jnp.exp(prolong(log_param))
+    trap_rate = density * prolong(jnp.exp(log_param))
     source = -TIME_STEP * trap_rate * background
-    tangent = source[None] * prolong(probe_dirs)
-    for step_index in range(STEPS - 1):
-        padded = padded_2(tangent, (("space", 1),), 1)
-        tangent = stencil(padded, tangent, trap_rate)
-    adjoint = tangent
-    summed = adjoint
-    for step_index in range(STEPS - 1):
-        padded = padded_2(adjoint, (("space", 1),), 1)
-        adjoint = stencil(padded, adjoint, trap_rate)
-        summed = summed + adjoint
-    images = restrict(source[None] * summed).reshape((probe_count, planes * plane_cells))
-    cell_count = float(planes * lax.axis_size("space") * plane_cells)
+
+    def my_share(part):
+        both = jnp.concatenate([trap_rate[part], source[part]], axis=0)
+        rows = both.reshape((-1, PX * REF))
+        length = rows.shape[0] // lax.axis_size("probe")
+        return lax.dynamic_slice_in_dim(rows, lax.axis_index("probe") * length, length, 0)
+
+    from_below = lax.ppermute(my_share(slice(REF - REACH, REF)), "space", up)
+    from_above = lax.ppermute(my_share(slice(0, REACH)), "space", down)
+    halo = lax.all_gather(jnp.stack([from_below, from_above]), "probe", axis=0)
+    dirs = jnp.concatenate(
+        [
+            lax.ppermute(probe_dirs, "space", up),
+            probe_dirs,
+            lax.ppermute(probe_dirs, "space", down),
+        ],
+        axis=1,
+    ).reshape((probe_count, 3, PY, PX))
+    edge = jnp.stack([slab > 0, slab < slabs - 1]).astype(jnp.float32)
+    images = window_images(edge, trap_rate, source, halo, dirs)
+    images = images.reshape((probe_count, planes * plane_cells))
+    cell_count = float(planes * slabs * plane_cells)
     q_local, lower_factor = orthogonalize(images, cell_count)
     return (q_local.reshape((probe_count, planes, plane_cells)), lower_factor)
 

time: 218 us -> 171 us (0.78)
  starting transfers between devices: 42.5 us -> 21.5 us
  other arithmetic: 23.8 us -> 3.64 us
  between operations: 0.89 us -> 14.2 us
  local copies, waits for them, and re-layouts: 16.8 us -> 7.93 us
  Pallas kernels: 89.8 us -> 83.7 us
  waiting for transfers between devices: 42.4 us -> 38.4 us
    pallas_call x1, Pallas kernels: 89.8 us -> 43.9 us  [orthogonalize(): pl.pallas_call(body, out_shape=(jax.ShapeDtypeStruct((count, cells), jnp....]
    pallas_call x0 -> x1, Pallas kernels: none -> 39.9 us  [window_images(): pl.pallas_call(window_kernel, out_shape=jax.ShapeDtypeStruct((dirs.shape[...]
    ppermute x12 -> x4, waiting for transfers between devices: 42.4 us -> 3.41 us  [the longest x1 1.45 us: shards(): from_above = lax.ppermute(my_share(slice(0, REACH)), 'space', down)]
    all_gather x0 -> x1, waiting for transfers between devices: none -> 35 us  [shards(): halo = lax.all_gather(jnp.stack([from_below, from_above]), 'probe', axis=0)]
    ppermute x12 -> x4, starting transfers between devices: 42.5 us -> 21.5 us  [the longest x1 8.85 us: shards(): from_above = lax.ppermute(my_share(slice(0, REACH)), 'space', down)]
    add x5 -> x0, other arithmetic: 12.2 us -> none  [stencil(): current + TIME_STEP * (up_down + lateral - 6.0 * current - trap_rate[None...]
    reduce_sum x2 -> x0, other arithmetic: 7.79 us -> none  [restrict(): jnp.sum(shaped, axis=(2, 4, 6)).reshape((probe_count, planes, PY * PX))]
    broadcast_in_dim x4 -> x3, local copies, waits for them, and re-layouts: 6.87 us -> 0.78 us  [prolong(): jnp.broadcast_to(coarse_grid[..., :, None, :, None, :, None], leading + (...]
  transfers between devices with their start and end apart: 12 -> 5, of which waited for: 12 -> 4; matrix products, arithmetic and copies ran while one was open for 0% -> 0% of each run, Pallas kernels for 0% -> 0%
where the time goes in v3:
time: 171 us; the launch traced here: 169 us
  Pallas kernels  83.7 us (49%)
  waiting for transfers between devices  38.4 us (22%)
  starting transfers between devices  21.5 us (13%)
  between operations  14.2 us (8%)
  local copies, waits for them, and re-layouts  7.93 us (5%)
  other arithmetic  3.64 us (2%)
    pallas_call x1, Pallas kernels, orthogonalize(): pl.pallas_call(body, out_shape=(jax.ShapeDtypeStruct((count, cells), jnp....  43.9 us
    pallas_call x1, Pallas kernels, window_images(): pl.pallas_call(window_kernel, out_shape=jax.ShapeDtypeStruct((dirs.shape[...  39.9 us
    all_gather x1, waiting for transfers between devices, shards(): halo = lax.all_gather(jnp.stack([from_below, from_above]), 'probe', axis=0)  35 us
    ppermute x1, starting transfers between devices, shards(): from_above = lax.ppermute(my_share(slice(0, REACH)), 'space', down)  8.85 us
    ppermute x1, starting transfers between devices, shards(): lax.ppermute(probe_dirs, 'space', down)  6.42 us
    ppermute x1, starting transfers between devices, shards(): from_below = lax.ppermute(my_share(slice(REF - REACH, REF)), 'space', up)  4.28 us
    unnamed x10, local copies, waits for them, and re-layouts  4.02 us
  transfers between devices with their start and end apart: 5, of which 4 were waited for; matrix products, arithmetic and copies ran while one was open for 0% of the time, Pallas kernels for 0%

profile of v3, /device:TPU:6, one launch (start us, length us, event | category | flops | bytes accessed | tf_op | source)
XLA Modules:
  0.0 169.4 jit_solution(12041007972183150217)
XLA Ops:
  7.2 0.0 copy-start.1
  7.2 0.0 copy-start.2
  7.2 0.0 all-gather.3.cloned.1.call-start
  7.2 1.4 fusion.2
  8.7 0.7 exponential_reduce_fusion
  9.4 0.1 broadcast_in_dim.36
  9.4 0.2 broadcast_in_dim.37
  9.6 0.5 broadcast_in_dim.38
  10.2 2.7 %multiply_multiply_fusion = (f32[8,32,512]{2,1,0:T(8,128)S(1)}, f32[8,32,512]{2,1,0:T(8,128)S(1)}) fusion(f32[8,32,512]{2,1,0:T(8,128)S(1)} %copy-done.1, f32[32,512]{1,0:T(8,128)S(1)} %broadcast_in_dim.38, f32[]{:T(128)} %bitcast.5, s32[8,32,512]{2,1,0:T(8,128)S(1)} %copy-done.2, f32[]{:T(128)} %bitcast.4, f32[]{:T(128)} %bitcast.3, f32[]{:T(128)} %bitcast.2), kind=kLoop, calls=%fused_computation.2 | loop fusion | flops 1835008 | bytes 2162704 | tf_op jit(solution)/shard_map/mul | solution.py:291
  12.9 0.2 fusion
  13.1 0.1 pad_maximum_fusion
  13.2 0.0 copy-start.3
  13.2 4.3 %collective-permute-start = (f32[48,512]{1,0:T(8,128)S(1)}, f32[48,512]{1,0:T(8,128)S(1)}, u32[]{:S(2)}, u32[]{:S(2)}) collective-permute-start(f32[48,512]{1,0:T(8,128)S(1)} %constant_dynamic-slice_fusion.1), channel_id=1, source_target_pairs={{0,1},{1,2},{2,3},{3,4},{4,5},{5,6},{6,7},{7,8},{8,9},{9,10},{10,1... | collective-permute-start | bytes 294920 | tf_op jit(solution)/shard_map/ppermute | solution.py:299
  17.5 0.1 pad_maximum_fusion.1
  17.6 8.9 %collective-permute-start.1 = (f32[48,512]{1,0:T(8,128)S(1)}, f32[48,512]{1,0:T(8,128)S(1)}, u32[]{:S(2)}, u32[]{:S(2)}) collective-permute-start(f32[48,512]{1,0:T(8,128)S(1)} %constant_dynamic-slice_fusion), channel_id=1, source_target_pairs={{1,0},{2,1},{3,2},{4,3},{5,4},{6,5},{7,6},{8,7},{9,8},{10,9},{11,1... | collective-permute-start | bytes 294920 | tf_op jit(solution)/shard_map/ppermute | solution.py:300
  26.5 0.7 collective-permute-done
  27.2 1.4 collective-permute-done.1
  28.7 0.7 pad_maximum_fusion.2
  29.3 0.0 all-gather.3.cloned.1.call-update
  29.4 1.9 %collective-permute-start.2 = (f32[4,1,256]{2,1,0:T(1,128)S(1)}, f32[4,1,256]{2,1,0:T(1,128)S(1)}, u32[]{:S(2)}, u32[]{:S(2)}) collective-permute-start(f32[4,1,256]{2,1,0:T(1,128)S(1)} %copy-done.3), channel_id=1, source_target_pairs={{0,1},{1,2},{2,3},{3,4},{4,5},{5,6},{6,7},{7,8},{8,9},{9,10},{10,1... | collective-permute-start | bytes 12296 | tf_op jit(solution)/shard_map/ppermute | solution.py:304
  31.3 6.4 %collective-permute-start.3 = (f32[4,1,256]{2,1,0:T(1,128)S(1)}, f32[4,1,256]{2,1,0:T(1,128)S(1)}, u32[]{:S(2)}, u32[]{:S(2)}) collective-permute-start(f32[4,1,256]{2,1,0:T(1,128)S(1)} %copy-done.3), channel_id=1, source_target_pairs={{1,0},{2,1},{3,2},{4,3},{5,4},{6,5},{7,6},{8,7},{9,8},{10,9},{11,1... | collective-permute-start | bytes 12296 | tf_op jit(solution)/shard_map/ppermute | solution.py:306
  37.7 0.1 add_convert_fusion.edge_ref
  37.8 0.0 collective-permute-done.2
  37.8 1.2 collective-permute-done.3
  39.1 0.1 reshape.26.dirs_ref
  39.2 35.0 %all-gather.3.cloned.1.call-done = f32[16,48,512]{2,1,0:T(8,128)} async-done(((f32[2,48,512]{2,1,0:T(8,128)}), f32[16,48,512]{2,1,0:T(8,128)}) %all-gather.3.cloned.1.call-update) | async-done | bytes 1572880 | tf_op jit(solution)/shard_map/all_gather | solution.py:301
  74.1 1.4 copy-done
  75.5 39.9 %shard_map.68 = f32[4,4,64]{2,1,0:T(4,128)S(1)} custom-call(f32[2]{0:T(128)S(1)} %add_convert_fusion.edge_ref, f32[8,32,512]{2,1,0:T(8,128)S(1)} %get-tuple-element.13.trap_ref, f32[8,32,512]{2,1,0:T(8,128)S(1)} %get-tuple-element.12.source_ref, f32[8,2,48,512]{3,2,1,0:T(8,128)S(1)} %bitcast.14, f32[4,3,4,64]{3,2,1,0:T(4,128)S(1)} %reshape.26.dirs_ref), custom_call_target="tpu_custom_call" | custom-call | tf_op jit(solution)/shard_map/pallas_call | solution.py:266
  115.4 0.7 reshape.27.refs_0_
  116.1 43.9 %shard_map.69 = (f32[4,256]{1,0:T(4,128)}, f32[32,32]{1,0:T(8,128)}) custom-call(f32[4,256]{1,0:T(4,128)} %reshape.27.refs_0_), custom_call_target="tpu_custom_call" | custom-call | tf_op jit(solution)/shard_map/pallas_call | solution.py:153
  160.0 1.3 copy.9
  161.3 1.3 copy.11
  (7 shorter events, 0.1 us)
Async XLA Ops:
  7.2 3.0 %copy-start.1 = (f32[8,32,512]{2,1,0:T(8,128)S(1)}, f32[8,32,512]{2,1,0:T(8,128)}, u32[]{:S(2)}) copy-start(f32[8,32,512]{2,1,0:T(8,128)} %param.7) | copy-start | bytes 1572868
  7.2 3.0 %copy-start.2 = (s32[8,32,512]{2,1,0:T(8,128)S(1)}, s32[8,32,512]{2,1,0:T(8,128)}, u32[]{:S(2)}) copy-start(s32[8,32,512]{2,1,0:T(8,128)} %param.8) | copy-start | bytes 1572868
  7.2 66.9 %all-gather.3.cloned.1.call-start = ((), (), s32[]{:S(2)}) async-start(), calls=%async_computation | async-start | bytes 1769472 | tf_op jit(solution)/shard_map/all_gather | solution.py:301
  13.2 16.2 %copy-start.3 = (f32[4,1,256]{2,1,0:T(1,128)S(1)}, f32[4,1,256]{2,1,0:T(1,128)}, u32[]{:S(2)}) copy-start(f32[4,1,256]{2,1,0:T(1,128)} %param.5) | copy-start | bytes 12292
  13.2 14.0 %collective-permute-start = (f32[48,512]{1,0:T(8,128)S(1)}, f32[48,512]{1,0:T(8,128)S(1)}, u32[]{:S(2)}, u32[]{:S(2)}) collective-permute-start(f32[48,512]{1,0:T(8,128)S(1)} %constant_dynamic-slice_fusion.1), channel_id=1, source_target_pairs={{0,1},{1,2},{2,3},{3,4},{4,5},{5,6},{6,7},{7,8},{8,9},{9,10},{10,1... | collective-permute-start | bytes 294920 | tf_op jit(solution)/shard_map/ppermute | solution.py:299
  17.6 11.1 %collective-permute-start.1 = (f32[48,512]{1,0:T(8,128)S(1)}, f32[48,512]{1,0:T(8,128)S(1)}, u32[]{:S(2)}, u32[]{:S(2)}) collective-permute-start(f32[48,512]{1,0:T(8,128)S(1)} %constant_dynamic-slice_fusion), channel_id=1, source_target_pairs={{1,0},{2,1},{3,2},{4,3},{5,4},{6,5},{7,6},{8,7},{9,8},{10,9},{11,1... | collective-permute-start | bytes 294920 | tf_op jit(solution)/shard_map/ppermute | solution.py:300
  29.4 8.4 %collective-permute-start.2 = (f32[4,1,256]{2,1,0:T(1,128)S(1)}, f32[4,1,256]{2,1,0:T(1,128)S(1)}, u32[]{:S(2)}, u32[]{:S(2)}) collective-permute-start(f32[4,1,256]{2,1,0:T(1,128)S(1)} %copy-done.3), channel_id=1, source_target_pairs={{0,1},{1,2},{2,3},{3,4},{4,5},{5,6},{6,7},{7,8},{8,9},{9,10},{10,1... | collective-permute-start | bytes 12296 | tf_op jit(solution)/shard_map/ppermute | solution.py:304
  31.3 7.7 %collective-permute-start.3 = (f32[4,1,256]{2,1,0:T(1,128)S(1)}, f32[4,1,256]{2,1,0:T(1,128)S(1)}, u32[]{:S(2)}, u32[]{:S(2)}) collective-permute-start(f32[4,1,256]{2,1,0:T(1,128)S(1)} %copy-done.3), channel_id=1, source_target_pairs={{1,0},{2,1},{3,2},{4,3},{5,4},{6,5},{7,6},{8,7},{9,8},{10,9},{11,1... | collective-permute-start | bytes 12296 | tf_op jit(solution)/shard_map/ppermute | solution.py:306
  74.1 1.4 copy-start
Sparse Core Ops, SparseCore 0:
  29.5 44.5 all-gather.2

commit v4 on v3

--- a/solution.py
+++ b/solution.py
@@ -178,7 +178,7 @@
 
 def window_kernel(
     edge_ref, trap_ref, source_ref, halo_ref, dirs_ref, images_ref, keep, source, first, second,
-    summed,
+    summed, wide, narrow,
 ):
     fine_y, fine_x = PY * REF, PX * REF
     share = halo_ref.shape[2] // CHUNK
@@ -206,9 +206,10 @@
     x_fine = lax.broadcasted_iota(jnp.int32, (PX, fine_x), 1)
     x_cell = lax.broadcasted_iota(jnp.int32, (PX, fine_x), 0)
     spread_x = jnp.where(x_fine // REF == x_cell, 1.0, 0.0)
-    y_fine = lax.broadcasted_iota(jnp.int32, (fine_y, PY), 0)
-    y_cell = lax.broadcasted_iota(jnp.int32, (fine_y, PY), 1)
-    spread_y = jnp.where(y_fine // REF == y_cell, 1.0, 0.0)
+    probes = dirs_ref.shape[0]
+    all_wide = dot_highest(dirs_ref[...].reshape((-1, PX)), spread_x, ((1,), (0,)))
+    for at in range(3 * PY * probes):
+        wide[at // PY, at % PY, :] = all_wide[at]
     row_at = lax.broadcasted_iota(jnp.int32, (fine_y, fine_x), 0)
     lane_at = lax.broadcasted_iota(jnp.int32, (fine_y, fine_x), 1)
 
@@ -227,19 +228,17 @@
             new = keep[i] * v + weight * around
             dst[i] = new
             if add:
-                @pl.when((i >= REACH) & (i < REACH + REF))
-                def _():
-                    at = i - REACH
-                    summed[at] = summed[at] + new
+                summed[i] = summed[i] + new
             return carry
 
-        lax.fori_loop(low, high, plane_step, 0)
+        lax.fori_loop(low, high, plane_step, 0, unroll=2)
 
     def probe_step(p, carry):
         for cell in range(3):
-            coarse = dirs_ref[p, cell]
-            wide = dot_highest(coarse, spread_x, ((1,), (0,)))
-            fine = dot_highest(spread_y, wide, ((1,), (0,)))
+            coarse = wide[3 * p + cell]
+            fine = jnp.concatenate(
+                [jnp.broadcast_to(coarse[y : y + 1], (REF, fine_x)) for y in range(PY)], axis=0
+            )
             low = max(0, REACH - REF + cell * REF)
             high = min(EXTENDED, REACH + cell * REF)
             for i in range(low, high):
@@ -249,15 +248,19 @@
             src, dst = bufs[(n - 1) % 2], bufs[n % 2]
             advance(src, dst, n, EXTENDED - n, n >= STEPS)
             if n == STEPS - 1:
-                summed[...] = dst[own]
-        total = source[REACH] * summed[0]
-        for at in range(1, REF):
-            total = total + source[REACH + at] * summed[at]
-        narrow = dot_highest(total, spread_x, ((1,), (1,)))
-        images_ref[p] = dot_highest(spread_y, narrow, ((0,), (0,)))
+                summed[own] = dst[own]
+        total = source[REACH] * summed[REACH]
+        for at in range(REACH + 1, REACH + REF):
+            total = total + source[at] * summed[at]
+        for y in range(PY):
+            narrow[p, y : y + 1, :] = jnp.sum(
+                total[y * REF : (y + 1) * REF], axis=0, keepdims=True
+            )
         return carry
 
-    lax.fori_loop(0, dirs_ref.shape[0], probe_step, 0)
+    lax.fori_loop(0, probes, probe_step, 0)
+    for p in range(probes):
+        images_ref[p] = dot_highest(narrow[p], spread_x, ((1,), (1,)))
 
 
 def window_images(edge, trap_rate, source, halo, dirs):
@@ -273,10 +276,133 @@
             pltpu.VMEM((EXTENDED,) + plane, jnp.float32),
             pltpu.VMEM((EXTENDED,) + plane, jnp.float32),
             pltpu.VMEM((EXTENDED,) + plane, jnp.float32),
-            pltpu.VMEM((REF,) + plane, jnp.float32),
+            pltpu.VMEM((EXTENDED,) + plane, jnp.float32),
+            pltpu.VMEM((3 * dirs.shape[0], PY, PX * REF), jnp.float32),
+            pltpu.VMEM((dirs.shape[0], PY, PX * REF), jnp.float32),
         ],
         compiler_params=pltpu.CompilerParams(vmem_limit_bytes=32 * 1024 * 1024),
     )(edge, trap_rate, source, halo, dirs)
+
+
+CHIPS = 4
+
+
+def halo_kernel(
+    up_ref, down_ref, halo_ref, cross_send, cross_recv, line_send, line_recv, pair_send, pair_recv
+):
+    mesh_id = pl.DeviceIdType.MESH
+    me = lax.axis_index("probe")
+    slab, slabs = lax.axis_index("space"), lax.axis_size("space")
+    core, chip = lax.rem(me, 2), lax.div(me, 2)
+    partner = {"probe": chip * 2 + 1 - core}
+    has_below, has_above = slab > 0, slab < slabs - 1
+
+    def line_slot(k):
+        return lax.rem(chip + k, CHIPS) * 2 + core
+
+    barrier = pltpu.get_barrier_semaphore()
+
+    def greet(device):
+        pl.semaphore_signal(barrier, inc=1, device_id=device, device_id_type=mesh_id)
+
+    for k in range(1, CHIPS):
+        greet({"probe": line_slot(k)})
+    greet(partner)
+
+    @pl.when(has_below)
+    def _():
+        greet({"space": slab - 1})
+
+    @pl.when(has_above)
+    def _():
+        greet({"space": slab + 1})
+
+    pl.semaphore_wait(
+        barrier, CHIPS + has_below.astype(jnp.int32) + has_above.astype(jnp.int32)
+    )
+
+    def send(src, dst, send_sem, recv_sem, device):
+        return pltpu.make_async_remote_copy(
+            src_ref=src, dst_ref=dst, send_sem=send_sem, recv_sem=recv_sem,
+            device_id=device, device_id_type=mesh_id,
+        )
+
+    def cross(side):
+        share, step = ((up_ref, 1), (down_ref, -1))[side]
+        return send(
+            share, halo_ref.at[me, side], cross_send.at[side], cross_recv.at[side],
+            {"space": slab + step},
+        )
+
+    goes, comes = (has_above, has_below), (has_below, has_above)
+    for side in range(2):
+
+        @pl.when(goes[side])
+        def _():
+            cross(side).start()
+
+    def line(side, slot, k):
+        return send(
+            halo_ref.at[slot, side], halo_ref.at[slot, side], line_send.at[side, k],
+            line_recv.at[side, slot], {"probe": line_slot(k)},
+        )
+
+    def pair(slot, k, at):
+        return send(
+            halo_ref.at[slot], halo_ref.at[slot], pair_send.at[k], pair_recv.at[at], partner
+        )
+
+    for side in range(2):
+
+        @pl.when(comes[side])
+        def _():
+            cross(side).wait_recv()
+
+        @pl.when(jnp.logical_not(comes[side]))
+        def _():
+            fill = pltpu.make_async_copy(
+                (up_ref, down_ref)[side], halo_ref.at[me, side], cross_recv.at[side]
+            )
+            fill.start()
+            fill.wait()
+
+        for k in range(1, CHIPS):
+            line(side, me, k).start()
+    pair(me, 0, chip).start()
+    for k in range(1, CHIPS):
+        slot = line_slot(k)
+        for side in range(2):
+            line(side, slot, k).wait_recv()
+        pair(slot, k, lax.div(slot, 2)).start()
+    for k in range(CHIPS):
+        from_chip = lax.rem(chip + k, CHIPS)
+        pair(from_chip * 2 + 1 - core, k, from_chip).wait_recv()
+    for side in range(2):
+
+        @pl.when(goes[side])
+        def _():
+            cross(side).wait_send()
+
+        for k in range(1, CHIPS):
+            line(side, me, k).wait_send()
+    for k in range(CHIPS):
+        pair(me, k, chip).wait_send()
+
+
+def exchange_halo(up_share, down_share):
+    vmem = pl.BlockSpec(memory_space=pltpu.VMEM)
+    dma = pltpu.SemaphoreType.DMA
+    return pl.pallas_call(
+        halo_kernel,
+        out_shape=jax.ShapeDtypeStruct((2 * CHIPS, 2) + up_share.shape, jnp.float32),
+        in_specs=[vmem, vmem],
+        out_specs=pl.BlockSpec(memory_space=pl.ANY),
+        scratch_shapes=[
+            dma((2,)), dma((2,)), dma((2, CHIPS)), dma((2, 2 * CHIPS)), dma((CHIPS,)),
+            dma((CHIPS,)),
+        ],
+        compiler_params=pltpu.CompilerParams(collective_id=1, has_side_effects=True),
+    )(up_share, down_share)
 
 
 def shards(probe_dirs, log_param, background, site_class, trap_density):
@@ -296,9 +422,7 @@
         length = rows.shape[0] // lax.axis_size("probe")
         return lax.dynamic_slice_in_dim(rows, lax.axis_index("probe") * length, length, 0)
 
-    from_below = lax.ppermute(my_share(slice(REF - REACH, REF)), "space", up)
-    from_above = lax.ppermute(my_share(slice(0, REACH)), "space", down)
-    halo = lax.all_gather(jnp.stack([from_below, from_above]), "probe", axis=0)
+    halo = exchange_halo(my_share(slice(REF - REACH, REF)), my_share(slice(0, REACH)))
     dirs = jnp.concatenate(
         [
             lax.ppermute(probe_dirs, "space", up),

time: 171 us -> 131 us (0.77)
  waiting for transfers between devices: 38.4 us -> 0.01 us
  Pallas kernels: 83.7 us -> 103 us
  between operations: 14.2 us -> 0.78 us
  starting transfers between devices: 21.5 us -> 13.3 us
    all_gather x1 -> x0, waiting for transfers between devices: 35 us -> none  [shards(): halo = lax.all_gather(jnp.stack([from_below, from_above]), 'probe', axis=0)]
    pallas_call x0 -> x1, Pallas kernels: none -> 28.5 us  [exchange_halo(): pl.pallas_call(halo_kernel, out_shape=jax.ShapeDtypeStruct((2 * CHIPS, 2)...]
    pallas_call x1, Pallas kernels: 39.9 us -> 24.4 us  [window_images(): pl.pallas_call(window_kernel, out_shape=jax.ShapeDtypeStruct((dirs.shape[...]
    ppermute x2 -> x0, starting transfers between devices: 13.1 us -> none  [the longest x1 8.85 us: shards(): from_above = lax.ppermute(my_share(slice(0, REACH)), 'space', down)]
    pallas_call x1, Pallas kernels: 43.9 us -> 50.6 us  [orthogonalize(): pl.pallas_call(body, out_shape=(jax.ShapeDtypeStruct((count, cells), jnp....]
    ppermute x1, starting transfers between devices: 1.92 us -> 4.41 us  [shards(): lax.ppermute(probe_dirs, 'space', up)]
    ppermute x1, starting transfers between devices: 6.42 us -> 8.86 us  [shards(): lax.ppermute(probe_dirs, 'space', down)]
    ppermute x2 -> x0, waiting for transfers between devices: 2.19 us -> none  [the longest x1 1.45 us: shards(): from_above = lax.ppermute(my_share(slice(0, REACH)), 'space', down)]
  transfers between devices with their start and end apart: 5 -> 2, of which waited for: 4 -> 0; matrix products, arithmetic and copies ran while one was open for 0% -> 6% of each run, Pallas kernels for 0% -> 22%
where the time goes in v4:
time: 131 us; the launch traced here: 130 us
  Pallas kernels  103 us (79%)
  starting transfers between devices  13.3 us (10%)
  local copies, waits for them, and re-layouts  9.26 us (7%)
  other arithmetic  2.99 us (2%)
    pallas_call x1, Pallas kernels, orthogonalize(): pl.pallas_call(body, out_shape=(jax.ShapeDtypeStruct((count, cells), jnp....  50.6 us
    pallas_call x1, Pallas kernels, exchange_halo(): pl.pallas_call(halo_kernel, out_shape=jax.ShapeDtypeStruct((2 * CHIPS, 2)...  28.5 us
    pallas_call x1, Pallas kernels, window_images(): pl.pallas_call(window_kernel, out_shape=jax.ShapeDtypeStruct((dirs.shape[...  24.4 us
    ppermute x1, starting transfers between devices, shards(): lax.ppermute(probe_dirs, 'space', down)  8.86 us
    ppermute x1, starting transfers between devices, shards(): lax.ppermute(probe_dirs, 'space', up)  4.41 us
    unnamed x10, local copies, waits for them, and re-layouts  4.02 us
    mul x1, other arithmetic, shards(): source = -TIME_STEP * trap_rate * background  2.77 us
  transfers between devices with their start and end apart: 2, of which 0 were waited for; matrix products, arithmetic and copies ran while one was open for 6% of the time, Pallas kernels for 22%

profile of v4, /device:TPU:6, one launch (start us, length us, event | category | flops | bytes accessed | tf_op | source)
XLA Modules:
  0.0 129.8 jit_solution(15635811116412776076)
XLA Ops:
  0.6 0.0 copy-start.1
  0.6 0.0 copy-start.2
  0.7 4.4 %collective-permute-start = (f32[4,1,256]{2,1,0:T(1,128)}, f32[4,1,256]{2,1,0:T(1,128)S(1)}, u32[]{:S(2)}, u32[]{:S(2)}) collective-permute-start(f32[4,1,256]{2,1,0:T(1,128)} %param.5), channel_id=1, source_target_pairs={{0,1},{1,2},{2,3},{3,4},{4,5},{5,6},{6,7},{7,8},{8,9},{9,10},{10,1... | collective-permute-start | bytes 12296 | tf_op jit(solution)/shard_map/ppermute | solution.py:428
  5.1 8.9 %collective-permute-start.1 = (f32[4,1,256]{2,1,0:T(1,128)}, f32[4,1,256]{2,1,0:T(1,128)S(1)}, u32[]{:S(2)}, u32[]{:S(2)}) collective-permute-start(f32[4,1,256]{2,1,0:T(1,128)} %param.5), channel_id=1, source_target_pairs={{1,0},{2,1},{3,2},{4,3},{5,4},{6,5},{7,6},{8,7},{9,8},{10,9},{11,1... | collective-permute-start | bytes 12296 | tf_op jit(solution)/shard_map/ppermute | solution.py:430
  13.9 1.5 %fusion.2 = (f32[1]{0:T(128)}, f32[1]{0:T(128)}, f32[1]{0:T(128)}, f32[1]{0:T(128)}) fusion(f32[4]{0:T(128)} %param.9), kind=kLoop, calls=%fused_computation.11 | loop fusion | bytes 32 | tf_op jit(solution)/shard_map/slice | solution.py:415
  15.4 0.7 exponential_reduce_fusion
  16.1 0.1 broadcast_in_dim.36
  16.2 0.2 broadcast_in_dim.37
  16.4 0.5 broadcast_in_dim.38
  16.9 0.0 copy-done.1
  16.9 0.0 copy-done.2
  16.9 2.8 %multiply_multiply_fusion = (f32[8,32,512]{2,1,0:T(8,128)S(1)}, f32[8,32,512]{2,1,0:T(8,128)S(1)}) fusion(f32[8,32,512]{2,1,0:T(8,128)S(1)} %copy-done.1, f32[32,512]{1,0:T(8,128)S(1)} %broadcast_in_dim.38, f32[]{:T(128)} %bitcast.5, s32[8,32,512]{2,1,0:T(8,128)S(1)} %copy-done.2, f32[]{:T(128)} %bitcast.4, f32[]{:T(128)} %bitcast.3, f32[]{:T(128)} %bitcast.2), kind=kLoop, calls=%fused_computation.2 | loop fusion | flops 1835008 | bytes 2162704 | tf_op jit(solution)/shard_map/mul | solution.py:417
  19.7 0.2 fusion
  19.9 0.1 pad_maximum_fusion.1
  20.0 0.7 constant_dynamic-slice_fusion.down_ref
  20.6 0.0 copy-start.3
  20.6 0.1 pad_maximum_fusion
  20.7 0.6 constant_dynamic-slice_fusion.1.up_ref
  21.4 0.1 add_convert_fusion.edge_ref
  21.4 28.5 %shard_map.68.halo_ref = f32[8,2,48,512]{3,2,1,0:T(8,128)} custom-call(f32[48,512]{1,0:T(8,128)} %constant_dynamic-slice_fusion.1.up_ref, f32[48,512]{1,0:T(8,128)} %constant_dynamic-slice_fusion.down_ref), custom_call_target="tpu_custom_call" | custom-call | tf_op jit(solution)/shard_map/pallas_call | solution.py:395
  49.9 0.0 collective-permute-done
  50.0 0.0 collective-permute-done.1
  50.0 0.0 copy-done.3
  50.0 0.1 reshape.26.dirs_ref
  50.1 0.0 copy-start
  50.1 1.4 %copy-done = f32[8,2,48,512]{3,2,1,0:T(8,128)S(1)} copy-done((f32[8,2,48,512]{3,2,1,0:T(8,128)S(1)}, f32[8,2,48,512]{3,2,1,0:T(8,128)}, u32[]{:S(2)}) %copy-start) | copy-done | bytes 1572888
  51.5 24.4 %shard_map.69 = f32[4,4,64]{2,1,0:T(4,128)S(1)} custom-call(f32[2]{0:T(128)S(1)} %add_convert_fusion.edge_ref, f32[8,32,512]{2,1,0:T(8,128)S(1)} %get-tuple-element.11.trap_ref, f32[8,32,512]{2,1,0:T(8,128)S(1)} %get-tuple-element.10.source_ref, f32[8,2,48,512]{3,2,1,0:T(8,128)S(1)} %copy-done, f32[4,3,4,64]{3,2,1,0:T(4,128)S(1)} %reshape.26.dirs_ref), custom_call_target="tpu_custom_call" | custom-call | tf_op jit(solution)/shard_map/pallas_call | solution.py:269
  75.9 0.7 reshape.27.refs_0_
  76.6 50.6 %shard_map.70 = (f32[4,256]{1,0:T(4,128)}, f32[32,32]{1,0:T(8,128)}) custom-call(f32[4,256]{1,0:T(4,128)} %reshape.27.refs_0_), custom_call_target="tpu_custom_call" | custom-call | tf_op jit(solution)/shard_map/pallas_call | solution.py:153
  127.2 1.3 copy.8
  128.4 1.3 %copy.10 = f32[32,32]{1,0:T(8,128)} copy(f32[32,32]{1,0:T(8,128)} %get-tuple-element.25) | data formatting | bytes 8192
  (1 shorter events, 0.0 us)
Async XLA Ops:
  0.6 16.3 %copy-start.1 = (f32[8,32,512]{2,1,0:T(8,128)S(1)}, f32[8,32,512]{2,1,0:T(8,128)}, u32[]{:S(2)}) copy-start(f32[8,32,512]{2,1,0:T(8,128)} %param.7) | copy-start | bytes 1572868
  0.6 16.3 %copy-start.2 = (s32[8,32,512]{2,1,0:T(8,128)S(1)}, s32[8,32,512]{2,1,0:T(8,128)}, u32[]{:S(2)}) copy-start(s32[8,32,512]{2,1,0:T(8,128)} %param.8) | copy-start | bytes 1572868
  0.7 49.3 %collective-permute-start = (f32[4,1,256]{2,1,0:T(1,128)}, f32[4,1,256]{2,1,0:T(1,128)S(1)}, u32[]{:S(2)}, u32[]{:S(2)}) collective-permute-start(f32[4,1,256]{2,1,0:T(1,128)} %param.5), channel_id=1, source_target_pairs={{0,1},{1,2},{2,3},{3,4},{4,5},{5,6},{6,7},{7,8},{8,9},{9,10},{10,1... | collective-permute-start | bytes 12296 | tf_op jit(solution)/shard_map/ppermute | solution.py:428
  5.1 44.9 %collective-permute-start.1 = (f32[4,1,256]{2,1,0:T(1,128)}, f32[4,1,256]{2,1,0:T(1,128)S(1)}, u32[]{:S(2)}, u32[]{:S(2)}) collective-permute-start(f32[4,1,256]{2,1,0:T(1,128)} %param.5), channel_id=1, source_target_pairs={{1,0},{2,1},{3,2},{4,3},{5,4},{6,5},{7,6},{8,7},{9,8},{10,9},{11,1... | collective-permute-start | bytes 12296 | tf_op jit(solution)/shard_map/ppermute | solution.py:430
  20.6 29.4 %copy-start.3 = (f32[4,1,256]{2,1,0:T(1,128)S(1)}, f32[4,1,256]{2,1,0:T(1,128)}, u32[]{:S(2)}) copy-start(f32[4,1,256]{2,1,0:T(1,128)} %param.5) | copy-start | bytes 12292
  50.1 1.4 %copy-start = (f32[8,2,48,512]{3,2,1,0:T(8,128)S(1)}, f32[8,2,48,512]{3,2,1,0:T(8,128)}, u32[]{:S(2)}) copy-start(f32[8,2,48,512]{3,2,1,0:T(8,128)} %shard_map.68.halo_ref) | copy-start | bytes 4718596

commit v5 on v4

--- a/solution.py
+++ b/solution.py
@@ -288,7 +288,8 @@
 
 
 def halo_kernel(
-    up_ref, down_ref, halo_ref, cross_send, cross_recv, line_send, line_recv, pair_send, pair_recv
+    up_ref, down_ref, own_dirs_ref, halo_ref, dirs_ref, cross_send, cross_recv, line_send,
+    line_recv, pair_send, pair_recv, dirs_send, dirs_recv,
 ):
     mesh_id = pl.DeviceIdType.MESH
     me = lax.axis_index("probe")
@@ -334,12 +335,19 @@
             {"space": slab + step},
         )
 
+    def cross_dirs(side):
+        return send(
+            own_dirs_ref, dirs_ref.at[side], dirs_send.at[side], dirs_recv.at[side],
+            {"space": slab + (1, -1)[side]},
+        )
+
     goes, comes = (has_above, has_below), (has_below, has_above)
     for side in range(2):
 
         @pl.when(goes[side])
         def _():
             cross(side).start()
+            cross_dirs(side).start()
 
     def line(side, slot, k):
         return send(
@@ -365,6 +373,9 @@
             )
             fill.start()
             fill.wait()
+            fill_dirs = pltpu.make_async_copy(own_dirs_ref, dirs_ref.at[side], dirs_recv.at[side])
+            fill_dirs.start()
+            fill_dirs.wait()
 
         for k in range(1, CHIPS):
             line(side, me, k).start()
@@ -379,9 +390,14 @@
         pair(from_chip * 2 + 1 - core, k, from_chip).wait_recv()
     for side in range(2):
 
+        @pl.when(comes[side])
+        def _():
+            cross_dirs(side).wait_recv()
+
         @pl.when(goes[side])
         def _():
             cross(side).wait_send()
+            cross_dirs(side).wait_send()
 
         for k in range(1, CHIPS):
             line(side, me, k).wait_send()
@@ -389,27 +405,28 @@
         pair(me, k, chip).wait_send()
 
 
-def exchange_halo(up_share, down_share):
+def exchange_halo(up_share, down_share, own_dirs):
     vmem = pl.BlockSpec(memory_space=pltpu.VMEM)
     dma = pltpu.SemaphoreType.DMA
     return pl.pallas_call(
         halo_kernel,
-        out_shape=jax.ShapeDtypeStruct((2 * CHIPS, 2) + up_share.shape, jnp.float32),
-        in_specs=[vmem, vmem],
-        out_specs=pl.BlockSpec(memory_space=pl.ANY),
+        out_shape=(
+            jax.ShapeDtypeStruct((2 * CHIPS, 2) + up_share.shape, jnp.float32),
+            jax.ShapeDtypeStruct((2,) + own_dirs.shape, jnp.float32),
+        ),
+        in_specs=[vmem, vmem, vmem],
+        out_specs=(pl.BlockSpec(memory_space=pl.ANY), pl.BlockSpec(memory_space=pl.ANY)),
         scratch_shapes=[
             dma((2,)), dma((2,)), dma((2, CHIPS)), dma((2, 2 * CHIPS)), dma((CHIPS,)),
-            dma((CHIPS,)),
+            dma((CHIPS,)), dma((2,)), dma((2,)),
         ],
         compiler_params=pltpu.CompilerParams(collective_id=1, has_side_effects=True),
-    )(up_share, down_share)
+    )(up_share, down_share, own_dirs)
 
 
 def shards(probe_dirs, log_param, background, site_class, trap_density):
     probe_count, planes, plane_cells = probe_dirs.shape
     slabs, slab = lax.axis_size("space"), lax.axis_index("space")
-    up = [(i, i + 1) for i in range(slabs - 1)]
-    down = [(j, i) for i, j in up]
     density = jnp.zeros(site_class.shape, jnp.float32)
     for class_index in range(trap_density.shape[0]):
         density = density + jnp.where(site_class == class_index, trap_density[class_index], 0.0)
@@ -422,15 +439,11 @@
         length = rows.shape[0] // lax.axis_size("probe")
         return lax.dynamic_slice_in_dim(rows, lax.axis_index("probe") * length, length, 0)
 
-    halo = exchange_halo(my_share(slice(REF - REACH, REF)), my_share(slice(0, REACH)))
-    dirs = jnp.concatenate(
-        [
-            lax.ppermute(probe_dirs, "space", up),
-            probe_dirs,
-            lax.ppermute(probe_dirs, "space", down),
-        ],
-        axis=1,
-    ).reshape((probe_count, 3, PY, PX))
+    own_dirs = probe_dirs.reshape((probe_count, plane_cells))
+    halo, near = exchange_halo(
+        my_share(slice(REF - REACH, REF)), my_share(slice(0, REACH)), own_dirs
+    )
+    dirs = jnp.stack([near[0], own_dirs, near[1]], axis=1).reshape((probe_count, 3, PY, PX))
     edge = jnp.stack([slab > 0, slab < slabs - 1]).astype(jnp.float32)
     images = window_images(edge, trap_rate, source, halo, dirs)
     images = images.reshape((probe_count, planes * plane_cells))

time: 131 us -> 124 us (0.947)
  starting transfers between devices: 13.3 us -> 0 us
  Pallas kernels: 103 us -> 109 us
  local copies, waits for them, and re-layouts: 9.26 us -> 10.7 us
    ppermute x2 -> x0, starting transfers between devices: 13.3 us -> none  [the longest x1 8.86 us: shards(): lax.ppermute(probe_dirs, 'space', down)]
    pallas_call x1, Pallas kernels: 28.5 us -> 35.5 us  [exchange_halo(): pl.pallas_call(halo_kernel, out_shape=(jax.ShapeDtypeStruct((2 * CHIPS, 2...]
    pallas_call x1, Pallas kernels: 50.6 us -> 48.8 us  [orthogonalize(): pl.pallas_call(body, out_shape=(jax.ShapeDtypeStruct((count, cells), jnp....]
    unnamed x10 -> x11, local copies, waits for them, and re-layouts: 4.02 us -> 4.62 us
  transfers between devices with their start and end apart: 2 -> 0, of which waited for: 0 -> 0; matrix products, arithmetic and copies ran while one was open for 6% -> 0% of each run, Pallas kernels for 22% -> 0%
where the time goes in v5:
time: 124 us; the launch traced here: 123 us
  Pallas kernels  109 us (88%)
  local copies, waits for them, and re-layouts  10.7 us (9%)
  other arithmetic  2.94 us (2%)
    pallas_call x1, Pallas kernels, orthogonalize(): pl.pallas_call(body, out_shape=(jax.ShapeDtypeStruct((count, cells), jnp....  48.8 us
    pallas_call x1, Pallas kernels, exchange_halo(): pl.pallas_call(halo_kernel, out_shape=(jax.ShapeDtypeStruct((2 * CHIPS, 2...  35.5 us
    pallas_call x1, Pallas kernels, window_images(): pl.pallas_call(window_kernel, out_shape=jax.ShapeDtypeStruct((dirs.shape[...  24.4 us
    unnamed x11, local copies, waits for them, and re-layouts  4.62 us
    mul x1, other arithmetic, shards(): source = -TIME_STEP * trap_rate * background  2.71 us

profile of v5, /device:TPU:6, one launch (start us, length us, event | category | flops | bytes accessed | tf_op | source)
XLA Modules:
  0.0 123.1 jit_solution(2235183103503598782)
XLA Ops:
  0.6 0.0 copy-start.1
  0.6 0.0 copy-start.2
  0.7 1.4 %fusion.3 = (f32[1]{0:T(128)}, f32[1]{0:T(128)}, f32[1]{0:T(128)}, f32[1]{0:T(128)}) fusion(f32[4]{0:T(128)} %param.9), kind=kLoop, calls=%fused_computation.13 | loop fusion | bytes 32 | tf_op jit(solution)/shard_map/slice | solution.py:432
  2.1 0.7 exponential_reduce_fusion
  2.8 0.1 broadcast_in_dim.36
  2.8 0.2 broadcast_in_dim.37
  3.0 0.5 broadcast_in_dim.38
  3.5 0.0 copy-done.1
  3.5 0.0 copy-done.2
  3.6 2.7 %multiply_multiply_fusion = (f32[8,32,512]{2,1,0:T(8,128)S(1)}, f32[8,32,512]{2,1,0:T(8,128)S(1)}) fusion(f32[8,32,512]{2,1,0:T(8,128)S(1)} %copy-done.1, f32[32,512]{1,0:T(8,128)S(1)} %broadcast_in_dim.38, f32[]{:T(128)} %bitcast.5, s32[8,32,512]{2,1,0:T(8,128)S(1)} %copy-done.2, f32[]{:T(128)} %bitcast.4, f32[]{:T(128)} %bitcast.3, f32[]{:T(128)} %bitcast.2), kind=kLoop, calls=%fused_computation.2 | loop fusion | flops 1835008 | bytes 2162704 | tf_op jit(solution)/shard_map/mul | solution.py:434
  6.3 0.2 fusion
  6.5 0.0 copy-start.3
  6.5 0.1 pad_maximum_fusion.1
  6.6 0.7 constant_dynamic-slice_fusion.down_ref
  7.2 0.1 pad_maximum_fusion
  7.3 0.6 constant_dynamic-slice_fusion.1.up_ref
  8.0 0.0 copy-done.3
  8.0 0.6 copy.11
  8.6 35.5 %shard_map.68 = (f32[8,2,48,512]{3,2,1,0:T(8,128)}, f32[2,4,256]{2,1,0:T(4,128)}) custom-call(f32[48,512]{1,0:T(8,128)} %constant_dynamic-slice_fusion.1.up_ref, f32[48,512]{1,0:T(8,128)} %constant_dynamic-slice_fusion.down_ref, f32[4,256]{1,0:T(4,128)} %bitcast.16), custom_call_target="tpu_custom_call" | custom-call | tf_op jit(solution)/shard_map/pallas_call | solution.py:411
  44.1 0.7 fusion.2
  44.8 0.1 stack.21
  44.9 0.1 stack.23
  45.0 0.1 stack.22
  45.1 0.1 add_convert_fusion.edge_ref
  45.2 0.0 copy-start
  45.2 1.4 %copy-done = f32[8,2,48,512]{3,2,1,0:T(8,128)S(1)} copy-done((f32[8,2,48,512]{3,2,1,0:T(8,128)S(1)}, f32[8,2,48,512]{3,2,1,0:T(8,128)}, u32[]{:S(2)}) %copy-start) | copy-done | bytes 1572888
  46.6 24.4 %shard_map.69 = f32[4,4,64]{2,1,0:T(4,128)S(1)} custom-call(f32[2]{0:T(128)S(1)} %add_convert_fusion.edge_ref, f32[8,32,512]{2,1,0:T(8,128)S(1)} %get-tuple-element.15.trap_ref, f32[8,32,512]{2,1,0:T(8,128)S(1)} %get-tuple-element.14.source_ref, f32[8,2,48,512]{3,2,1,0:T(8,128)S(1)} %copy-done, f32[4,3,4,64]{3,2,1,0:T(4,128)S(1)} %pad_maximum_fusion.2.dirs_ref), custom_call_target="tpu_custom_call" | custom-call | tf_op jit(solution)/shard_map/pallas_call | solution.py:269
  71.0 0.7 reshape.33.refs_0_
  71.7 48.8 %shard_map.70 = (f32[4,256]{1,0:T(4,128)}, f32[32,32]{1,0:T(8,128)}) custom-call(f32[4,256]{1,0:T(4,128)} %reshape.33.refs_0_), custom_call_target="tpu_custom_call" | custom-call | tf_op jit(solution)/shard_map/pallas_call | solution.py:153
  120.5 1.3 %copy.8 = f32[4,1,256]{2,1,0:T(1,128)} copy(f32[4,1,256]{2,0,1:T(4,128)} %bitcast.17) | data formatting | bytes 8192
  121.8 1.3 %copy.13 = f32[32,32]{1,0:T(8,128)} copy(f32[32,32]{1,0:T(8,128)} %get-tuple-element.31) | data formatting | bytes 8192
  (2 shorter events, 0.0 us)
Async XLA Ops:
  0.6 2.9 %copy-start.1 = (f32[8,32,512]{2,1,0:T(8,128)S(1)}, f32[8,32,512]{2,1,0:T(8,128)}, u32[]{:S(2)}) copy-start(f32[8,32,512]{2,1,0:T(8,128)} %param.7) | copy-start | bytes 1572868
  0.6 2.9 %copy-start.2 = (s32[8,32,512]{2,1,0:T(8,128)S(1)}, s32[8,32,512]{2,1,0:T(8,128)}, u32[]{:S(2)}) copy-start(s32[8,32,512]{2,1,0:T(8,128)} %param.8) | copy-start | bytes 1572868
  6.5 1.5 %copy-start.3 = (f32[4,1,256]{2,1,0:T(1,128)S(1)}, f32[4,1,256]{2,1,0:T(1,128)}, u32[]{:S(2)}) copy-start(f32[4,1,256]{2,1,0:T(1,128)} %param.5) | copy-start | bytes 12292
  45.2 1.4 %copy-start = (f32[8,2,48,512]{3,2,1,0:T(8,128)S(1)}, f32[8,2,48,512]{3,2,1,0:T(8,128)}, u32[]{:S(2)}) copy-start(f32[8,2,48,512]{3,2,1,0:T(8,128)} %get-tuple-element.6.halo_ref) | copy-start | bytes 4718596

commit v6 on v5

--- a/solution.py
+++ b/solution.py
@@ -214,11 +214,12 @@
     lane_at = lax.broadcasted_iota(jnp.int32, (fine_y, fine_x), 1)
 
     def advance(src, dst, low, high, add):
-        def plane_step(i, carry):
-            below = (i >= REACH).astype(jnp.float32)
-            above = (i < REACH + REF).astype(jnp.float32)
-            weight = TIME_STEP * (below + (1.0 - below) * edge_ref[0])
-            weight = weight * (above + (1.0 - above) * edge_ref[1])
+        for i in range(low, high):
+            weight = TIME_STEP
+            if i < REACH:
+                weight = TIME_STEP * edge_ref[0]
+            elif i >= REACH + REF:
+                weight = TIME_STEP * edge_ref[1]
             v = src[i]
             around = src[i - 1] + src[i + 1]
             around += jnp.where(row_at == 0, 0.0, pltpu.roll(v, 1, 0))
@@ -227,11 +228,8 @@
             around += jnp.where(lane_at == fine_x - 1, 0.0, pltpu.roll(v, fine_x - 1, 1))
             new = keep[i] * v + weight * around
             dst[i] = new
-            if add:
+            if add and REACH <= i < REACH + REF:
                 summed[i] = summed[i] + new
-            return carry
-
-        lax.fori_loop(low, high, plane_step, 0, unroll=2)
 
     def probe_step(p, carry):
         for cell in range(3):

time: 124 us -> 114 us (0.919)
  Pallas kernels: 109 us -> 98.8 us
    pallas_call x1, Pallas kernels: 24.4 us -> 14.4 us  [window_images(): pl.pallas_call(window_kernel, out_shape=jax.ShapeDtypeStruct((dirs.shape[...]
where the time goes in v6:
time: 114 us; the launch traced here: 113 us
  Pallas kernels  98.8 us (87%)
  local copies, waits for them, and re-layouts  10.7 us (9%)
  other arithmetic  2.94 us (3%)
    pallas_call x1, Pallas kernels, orthogonalize(): pl.pallas_call(body, out_shape=(jax.ShapeDtypeStruct((count, cells), jnp....  48.8 us
    pallas_call x1, Pallas kernels, exchange_halo(): pl.pallas_call(halo_kernel, out_shape=(jax.ShapeDtypeStruct((2 * CHIPS, 2...  35.5 us
    pallas_call x1, Pallas kernels, window_images(): pl.pallas_call(window_kernel, out_shape=jax.ShapeDtypeStruct((dirs.shape[...  14.4 us
    unnamed x11, local copies, waits for them, and re-layouts  4.62 us
    mul x1, other arithmetic, shards(): source = -TIME_STEP * trap_rate * background  2.71 us

profile of v6, /device:TPU:6, one launch (start us, length us, event | category | flops | bytes accessed | tf_op | source)
XLA Modules:
  0.0 113.2 jit_solution(9336081324522048521)
XLA Ops:
  0.6 0.0 copy-start.1
  0.6 0.0 copy-start.2
  0.7 1.4 %fusion.3 = (f32[1]{0:T(128)}, f32[1]{0:T(128)}, f32[1]{0:T(128)}, f32[1]{0:T(128)}) fusion(f32[4]{0:T(128)} %param.9), kind=kLoop, calls=%fused_computation.13 | loop fusion | bytes 32 | tf_op jit(solution)/shard_map/slice | solution.py:430
  2.1 0.7 exponential_reduce_fusion
  2.8 0.1 broadcast_in_dim.36
  2.8 0.2 broadcast_in_dim.37
  3.0 0.5 broadcast_in_dim.38
  3.5 0.0 copy-done.1
  3.5 0.0 copy-done.2
  3.6 2.7 %multiply_multiply_fusion = (f32[8,32,512]{2,1,0:T(8,128)S(1)}, f32[8,32,512]{2,1,0:T(8,128)S(1)}) fusion(f32[8,32,512]{2,1,0:T(8,128)S(1)} %copy-done.1, f32[32,512]{1,0:T(8,128)S(1)} %broadcast_in_dim.38, f32[]{:T(128)} %bitcast.5, s32[8,32,512]{2,1,0:T(8,128)S(1)} %copy-done.2, f32[]{:T(128)} %bitcast.4, f32[]{:T(128)} %bitcast.3, f32[]{:T(128)} %bitcast.2), kind=kLoop, calls=%fused_computation.2 | loop fusion | flops 1835008 | bytes 2162704 | tf_op jit(solution)/shard_map/mul | solution.py:432
  6.3 0.2 fusion
  6.5 0.0 copy-start.3
  6.5 0.1 pad_maximum_fusion.1
  6.6 0.7 constant_dynamic-slice_fusion.down_ref
  7.2 0.1 pad_maximum_fusion
  7.3 0.6 constant_dynamic-slice_fusion.1.up_ref
  8.0 0.0 copy-done.3
  8.0 0.6 copy.11
  8.6 35.5 %shard_map.68 = (f32[8,2,48,512]{3,2,1,0:T(8,128)}, f32[2,4,256]{2,1,0:T(4,128)}) custom-call(f32[48,512]{1,0:T(8,128)} %constant_dynamic-slice_fusion.1.up_ref, f32[48,512]{1,0:T(8,128)} %constant_dynamic-slice_fusion.down_ref, f32[4,256]{1,0:T(4,128)} %bitcast.16), custom_call_target="tpu_custom_call" | custom-call | tf_op jit(solution)/shard_map/pallas_call | solution.py:409
  44.1 0.7 fusion.2
  44.8 0.1 stack.21
  44.9 0.1 stack.23
  45.0 0.1 stack.22
  45.1 0.1 add_convert_fusion.edge_ref
  45.2 0.0 copy-start
  45.2 1.4 %copy-done = f32[8,2,48,512]{3,2,1,0:T(8,128)S(1)} copy-done((f32[8,2,48,512]{3,2,1,0:T(8,128)S(1)}, f32[8,2,48,512]{3,2,1,0:T(8,128)}, u32[]{:S(2)}) %copy-start) | copy-done | bytes 1572888
  46.6 14.4 %shard_map.69 = f32[4,4,64]{2,1,0:T(4,128)S(1)} custom-call(f32[2]{0:T(128)S(1)} %add_convert_fusion.edge_ref, f32[8,32,512]{2,1,0:T(8,128)S(1)} %get-tuple-element.15.trap_ref, f32[8,32,512]{2,1,0:T(8,128)S(1)} %get-tuple-element.14.source_ref, f32[8,2,48,512]{3,2,1,0:T(8,128)S(1)} %copy-done, f32[4,3,4,64]{3,2,1,0:T(4,128)S(1)} %pad_maximum_fusion.2.dirs_ref), custom_call_target="tpu_custom_call" | custom-call | tf_op jit(solution)/shard_map/pallas_call | solution.py:267
  61.0 0.7 reshape.33.refs_0_
  61.7 48.8 %shard_map.70 = (f32[4,256]{1,0:T(4,128)}, f32[32,32]{1,0:T(8,128)}) custom-call(f32[4,256]{1,0:T(4,128)} %reshape.33.refs_0_), custom_call_target="tpu_custom_call" | custom-call | tf_op jit(solution)/shard_map/pallas_call | solution.py:153
  110.6 1.3 %copy.8 = f32[4,1,256]{2,1,0:T(1,128)} copy(f32[4,1,256]{2,0,1:T(4,128)} %bitcast.17) | data formatting | bytes 8192
  111.8 1.3 %copy.13 = f32[32,32]{1,0:T(8,128)} copy(f32[32,32]{1,0:T(8,128)} %get-tuple-element.31) | data formatting | bytes 8192
  (2 shorter events, 0.0 us)
Async XLA Ops:
  0.6 2.9 %copy-start.1 = (f32[8,32,512]{2,1,0:T(8,128)S(1)}, f32[8,32,512]{2,1,0:T(8,128)}, u32[]{:S(2)}) copy-start(f32[8,32,512]{2,1,0:T(8,128)} %param.7) | copy-start | bytes 1572868
  0.6 2.9 %copy-start.2 = (s32[8,32,512]{2,1,0:T(8,128)S(1)}, s32[8,32,512]{2,1,0:T(8,128)}, u32[]{:S(2)}) copy-start(s32[8,32,512]{2,1,0:T(8,128)} %param.8) | copy-start | bytes 1572868
  6.5 1.5 %copy-start.3 = (f32[4,1,256]{2,1,0:T(1,128)S(1)}, f32[4,1,256]{2,1,0:T(1,128)}, u32[]{:S(2)}) copy-start(f32[4,1,256]{2,1,0:T(1,128)} %param.5) | copy-start | bytes 12292
  45.2 1.4 %copy-start = (f32[8,2,48,512]{3,2,1,0:T(8,128)S(1)}, f32[8,2,48,512]{3,2,1,0:T(8,128)}, u32[]{:S(2)}) copy-start(f32[8,2,48,512]{3,2,1,0:T(8,128)} %get-tuple-element.6.halo_ref) | copy-start | bytes 4718596

commit v7 on v6

--- a/solution.py
+++ b/solution.py
@@ -210,7 +210,7 @@
     all_wide = dot_highest(dirs_ref[...].reshape((-1, PX)), spread_x, ((1,), (0,)))
     for at in range(3 * PY * probes):
         wide[at // PY, at % PY, :] = all_wide[at]
-    row_at = lax.broadcasted_iota(jnp.int32, (fine_y, fine_x), 0)
+    edge_row = jnp.zeros((1, fine_x), jnp.float32)
     lane_at = lax.broadcasted_iota(jnp.int32, (fine_y, fine_x), 1)
 
     def advance(src, dst, low, high, add):
@@ -222,8 +222,8 @@
                 weight = TIME_STEP * edge_ref[1]
             v = src[i]
             around = src[i - 1] + src[i + 1]
-            around += jnp.where(row_at == 0, 0.0, pltpu.roll(v, 1, 0))
-            around += jnp.where(row_at == fine_y - 1, 0.0, pltpu.roll(v, fine_y - 1, 0))
+            around += jnp.concatenate([edge_row, src[i, : fine_y - 1, :]], axis=0)
+            around += jnp.concatenate([src[i, 1:, :], edge_row], axis=0)
             around += jnp.where(lane_at == 0, 0.0, pltpu.roll(v, 1, 1))
             around += jnp.where(lane_at == fine_x - 1, 0.0, pltpu.roll(v, fine_x - 1, 1))
             new = keep[i] * v + weight * around

time: 114 us -> 113 us (level)
  no operation moved by 1% of the time
where the time goes in v7:
time: 113 us; the launch traced here: 112 us
  Pallas kernels  97.9 us (87%)
  local copies, waits for them, and re-layouts  10.7 us (9%)
  other arithmetic  2.94 us (3%)
    pallas_call x1, Pallas kernels, orthogonalize(): pl.pallas_call(body, out_shape=(jax.ShapeDtypeStruct((count, cells), jnp....  48.8 us
    pallas_call x1, Pallas kernels, exchange_halo(): pl.pallas_call(halo_kernel, out_shape=(jax.ShapeDtypeStruct((2 * CHIPS, 2...  35.5 us
    pallas_call x1, Pallas kernels, window_images(): pl.pallas_call(window_kernel, out_shape=jax.ShapeDtypeStruct((dirs.shape[...  13.5 us
    unnamed x11, local copies, waits for them, and re-layouts  4.62 us
    mul x1, other arithmetic, shards(): source = -TIME_STEP * trap_rate * background  2.71 us

profile of v7, /device:TPU:6, one launch (start us, length us, event | category | flops | bytes accessed | tf_op | source)
XLA Modules:
  0.0 112.2 jit_solution(16061131743618642674)
XLA Ops:
  0.6 0.0 copy-start.1
  0.6 0.0 copy-start.2
  0.7 1.4 %fusion.3 = (f32[1]{0:T(128)}, f32[1]{0:T(128)}, f32[1]{0:T(128)}, f32[1]{0:T(128)}) fusion(f32[4]{0:T(128)} %param.9), kind=kLoop, calls=%fused_computation.13 | loop fusion | bytes 32 | tf_op jit(solution)/shard_map/slice | solution.py:430
  2.1 0.7 exponential_reduce_fusion
  2.8 0.1 broadcast_in_dim.36
  2.8 0.2 broadcast_in_dim.37
  3.0 0.5 broadcast_in_dim.38
  3.5 0.0 copy-done.1
  3.5 0.0 copy-done.2
  3.6 2.7 %multiply_multiply_fusion = (f32[8,32,512]{2,1,0:T(8,128)S(1)}, f32[8,32,512]{2,1,0:T(8,128)S(1)}) fusion(f32[8,32,512]{2,1,0:T(8,128)S(1)} %copy-done.1, f32[32,512]{1,0:T(8,128)S(1)} %broadcast_in_dim.38, f32[]{:T(128)} %bitcast.5, s32[8,32,512]{2,1,0:T(8,128)S(1)} %copy-done.2, f32[]{:T(128)} %bitcast.4, f32[]{:T(128)} %bitcast.3, f32[]{:T(128)} %bitcast.2), kind=kLoop, calls=%fused_computation.2 | loop fusion | flops 1835008 | bytes 2162704 | tf_op jit(solution)/shard_map/mul | solution.py:432
  6.3 0.2 fusion
  6.5 0.0 copy-start.3
  6.5 0.1 pad_maximum_fusion.1
  6.6 0.7 constant_dynamic-slice_fusion.down_ref
  7.2 0.1 pad_maximum_fusion
  7.3 0.6 constant_dynamic-slice_fusion.1.up_ref
  8.0 0.0 copy-done.3
  8.0 0.6 copy.11
  8.6 35.5 %shard_map.68 = (f32[8,2,48,512]{3,2,1,0:T(8,128)}, f32[2,4,256]{2,1,0:T(4,128)}) custom-call(f32[48,512]{1,0:T(8,128)} %constant_dynamic-slice_fusion.1.up_ref, f32[48,512]{1,0:T(8,128)} %constant_dynamic-slice_fusion.down_ref, f32[4,256]{1,0:T(4,128)} %bitcast.16), custom_call_target="tpu_custom_call" | custom-call | tf_op jit(solution)/shard_map/pallas_call | solution.py:409
  44.1 0.7 fusion.2
  44.8 0.1 stack.21
  44.9 0.1 stack.23
  45.0 0.1 stack.22
  45.1 0.1 add_convert_fusion.edge_ref
  45.2 0.0 copy-start
  45.2 1.4 %copy-done = f32[8,2,48,512]{3,2,1,0:T(8,128)S(1)} copy-done((f32[8,2,48,512]{3,2,1,0:T(8,128)S(1)}, f32[8,2,48,512]{3,2,1,0:T(8,128)}, u32[]{:S(2)}) %copy-start) | copy-done | bytes 1572888
  46.6 13.5 %shard_map.69 = f32[4,4,64]{2,1,0:T(4,128)S(1)} custom-call(f32[2]{0:T(128)S(1)} %add_convert_fusion.edge_ref, f32[8,32,512]{2,1,0:T(8,128)S(1)} %get-tuple-element.15.trap_ref, f32[8,32,512]{2,1,0:T(8,128)S(1)} %get-tuple-element.14.source_ref, f32[8,2,48,512]{3,2,1,0:T(8,128)S(1)} %copy-done, f32[4,3,4,64]{3,2,1,0:T(4,128)S(1)} %pad_maximum_fusion.2.dirs_ref), custom_call_target="tpu_custom_call" | custom-call | tf_op jit(solution)/shard_map/pallas_call | solution.py:267
  60.1 0.7 reshape.33.refs_0_
  60.8 48.8 %shard_map.70 = (f32[4,256]{1,0:T(4,128)}, f32[32,32]{1,0:T(8,128)}) custom-call(f32[4,256]{1,0:T(4,128)} %reshape.33.refs_0_), custom_call_target="tpu_custom_call" | custom-call | tf_op jit(solution)/shard_map/pallas_call | solution.py:153
  109.6 1.3 %copy.8 = f32[4,1,256]{2,1,0:T(1,128)} copy(f32[4,1,256]{2,0,1:T(4,128)} %bitcast.17) | data formatting | bytes 8192
  110.9 1.3 %copy.13 = f32[32,32]{1,0:T(8,128)} copy(f32[32,32]{1,0:T(8,128)} %get-tuple-element.31) | data formatting | bytes 8192
  (2 shorter events, 0.0 us)
Async XLA Ops:
  0.6 2.9 %copy-start.1 = (f32[8,32,512]{2,1,0:T(8,128)S(1)}, f32[8,32,512]{2,1,0:T(8,128)}, u32[]{:S(2)}) copy-start(f32[8,32,512]{2,1,0:T(8,128)} %param.7) | copy-start | bytes 1572868
  0.6 2.9 %copy-start.2 = (s32[8,32,512]{2,1,0:T(8,128)S(1)}, s32[8,32,512]{2,1,0:T(8,128)}, u32[]{:S(2)}) copy-start(s32[8,32,512]{2,1,0:T(8,128)} %param.8) | copy-start | bytes 1572868
  6.5 1.5 %copy-start.3 = (f32[4,1,256]{2,1,0:T(1,128)S(1)}, f32[4,1,256]{2,1,0:T(1,128)}, u32[]{:S(2)}) copy-start(f32[4,1,256]{2,1,0:T(1,128)} %param.5) | copy-start | bytes 12292
  45.2 1.4 %copy-start = (f32[8,2,48,512]{3,2,1,0:T(8,128)S(1)}, f32[8,2,48,512]{3,2,1,0:T(8,128)}, u32[]{:S(2)}) copy-start(f32[8,2,48,512]{3,2,1,0:T(8,128)} %get-tuple-element.6.halo_ref) | copy-start | bytes 4718596
